TPU v7x, 256 devices: a whole 4x4x8 slice. The times are simulated.
256 devices in a mesh: expert: 32 (over x, z), seq: 4 (over y_lo, core), fsdp: 2 (over y_hi).
Axes of the slice: x: 4, y: 4 (y_hi: 2, y_lo: 2; y = y_hi * 2 + y_lo), z: 8, core: 2. Of those that a mesh axis runs over, the one named last changes fastest.
Arguments:
- tokens: float32 [57344, 1280], P(('expert', 'seq', 'fsdp')), may hold values from -100 to 100
- slot_params: float32 [1280, 256], replicated, may hold values from -4 to 4
- w_in: float32 [64, 2560, 1280], P('expert', ('seq', 'fsdp')), may hold values from -0.15625 to 0.15625
- w_out: float32 [64, 2560, 1280], P('expert', ('seq', 'fsdp')), may hold values from -0.125 to 0.125
Outputs:
- mixed: float32 [57344, 1280], P(('expert', 'seq', 'fsdp'))
All inputs are finite; a program needn't handle non-finite values.
Results may differ from a plain program's by a relative error of at most 0.0003.
Values sent between devices are 32-bit elements; how exact they have to be, the bound alone decides.
A program may use at most 64 MiB of HBM per device.

v0:
```python
import functools

import jax
import jax.numpy as jnp
from jax import lax
from jax.sharding import Mesh
from jax.sharding import PartitionSpec as P

D = 1280
SLOTS = 4
EXPERT_SEQ_FSDP = ("expert_0", "expert_1", "seq_0", "seq_1", "fsdp")
EXPERT = ("expert_0", "expert_1")
SEQ_FSDP = ("seq_0", "seq_1", "fsdp")


def one_axis_at_a_time(array, axes):
    return functools.reduce(lax.pmax, axes, array)


def in_blocks(array, dim, devices):
    lengths = array.shape
    blocks = array.reshape(*lengths[:dim], devices, lengths[dim] // devices, *lengths[dim + 1 :])
    return jnp.moveaxis(blocks, dim, 0)


def summed_on_arrival(array, axis, dim):
    devices = lax.axis_size(axis)
    blocks = lax.all_to_all(in_blocks(array, dim, devices), axis, 0, 0, tiled=True)
    return jnp.sum(blocks, axis=0)


def side_by_side(arrays, axis, dim, along):
    columns = [a.reshape(*a.shape[:along], -1) for a in arrays]
    both = jnp.concatenate(columns, axis=along)
    whole, at, done = (summed_on_arrival(both, axis, dim), 0, [])
    for a, column in zip(arrays, columns):
        section = whole[..., at : at + column.shape[along]]
        done.append(section.reshape(*section.shape[:along], *a.shape[along:]))
        at += column.shape[along]
    return tuple(done)


def sent_to_all(array, axis):
    copies = jnp.broadcast_to(array, (lax.axis_size(axis), *array.shape))
    return lax.all_to_all(copies, axis, split_axis=0, concat_axis=0, tiled=True)


def over_copies(array, axis):
    everything = sent_to_all(array, axis)
    return jnp.sum(everything, axis=0)


def packed_total(arrays, axis):
    ends = [0]
    for a in arrays:
        ends.append(ends[-1] + a.size)
    total = over_copies(jnp.concatenate([a.ravel() for a in arrays]), axis)
    return tuple((total[b:e].reshape(a.shape) for a, b, e in zip(arrays, ends, ends[1:])))


def laid_out(blocks, dim):
    lengths = list(blocks.shape[1:])
    lengths[dim] *= blocks.shape[0]
    return jnp.moveaxis(blocks, 0, dim).reshape(lengths)


def gather_directly(array, axis, dim):
    blocks = sent_to_all(array, axis)
    return laid_out(blocks, dim)


def slot_terms(logits, tokens, slot_peak):
    weights = jnp.exp(logits - slot_peak)
    slot_mass = jnp.sum(weights, axis=0)
    slot_sums = lax.dot_general(
        weights,
        tokens,
        (((0,), (0,)), ((), ())),
        precision=lax.Precision.HIGHEST,
        preferred_element_type=jnp.float32,
    )
    return (slot_mass, slot_sums)


def body(tokens, slot_params, w_in, w_out):
    highest = lax.Precision.HIGHEST
    logits = jnp.dot(tokens, slot_params, precision=highest, preferred_element_type=jnp.float32)
    row_peak = jnp.max(logits, axis=1, keepdims=True)
    row_exp = jnp.exp(logits - row_peak)
    combine = row_exp / jnp.sum(row_exp, axis=1, keepdims=True)
    own_slots = w_in.shape[0] * SLOTS
    local_peak = jnp.max(logits, axis=0)
    slot_peak = one_axis_at_a_time(local_peak, EXPERT_SEQ_FSDP)
    slot_mass, slot_sums = slot_terms(logits, tokens, slot_peak)
    sums_own, mass_own = side_by_side((slot_sums, slot_mass), EXPERT, 0, 1)
    sums_own, mass_own = packed_total((sums_own, mass_own), SEQ_FSDP)
    slot_inputs = (sums_own / mass_own[:, None]).reshape(w_in.shape[0], SLOTS, D)
    hidden = jax.nn.gelu(
        jnp.einsum("esd,ehd->esh", slot_inputs, w_in, precision=highest), approximate=False
    )
    partial_out = jnp.einsum("esh,ehd->esd", hidden, w_out, precision=highest).reshape(own_slots, D)
    outputs_own = over_copies(partial_out, SEQ_FSDP)
    return jnp.dot(
        combine,
        gather_directly(outputs_own, EXPERT, 0),
        precision=lax.Precision.HIGHEST,
        preferred_element_type=jnp.float32,
    )


def solution(mesh):
    torus = Mesh(
        mesh.devices.reshape(4, 8, 2, 2, mesh.shape["fsdp"]),
        ("expert_0", "expert_1", "seq_0", "seq_1", "fsdp"),
    )
    return jax.shard_map(
        body,
        mesh=torus,
        in_specs=(
            P(EXPERT_SEQ_FSDP, None),
            P(),
            P(EXPERT, SEQ_FSDP, None),
            P(EXPERT, SEQ_FSDP, None),
        ),
        out_specs=P(EXPERT_SEQ_FSDP, None),
        check_vma=False,
    )
```

profile of v0, /device:TPU:1, one launch (start us, length us, event | category | flops | bytes accessed | tf_op | source)
XLA Modules:
  0.0 176.5 jit_solution(16315100795705798640)
XLA Ops:
  0.0 3.0 %fusion.127 = (f32[224]{0:T(256)S(1)}, f32[256]{0:T(256)S(1)}, f32[224,256]{1,0:T(8,128)S(1)}) fusion(f32[224,1280]{1,0:T(8,128)} %param.4, f32[1280,256]{1,0:T(8,128)} %param.5), kind=kOutput, calls=%fused_computation.144 | convolution fusion | flops 880918016 | bytes 2688896 | tf_op jit(solution)/shard_map/dot_general | solution.py:87
  3.0 9.3 %pmax.35 = f32[256]{0:T(256)S(1)} all-reduce(f32[256]{0:T(256)S(1)} %get-tuple-element.8), channel_id=1, replica_groups=mesh['expert_0'=4,'expert_1'=8,'seq_0'=2,'seq_1'=2,'fsdp'=2] {'expert_0'}, use_global_device_ids=true, to_apply=%region_3.0 | all-reduce | flops 256 | bytes 2048 | tf_op jit(solution)/shard_map/pmax | solution.py:17
  12.3 16.2 %pmax.36 = f32[256]{0:T(256)S(1)} all-reduce(f32[256]{0:T(256)S(1)} %pmax.35), channel_id=1, replica_groups=mesh['expert_0'=4,'expert_1'=8,'seq_0'=2,'seq_1'=2,'fsdp'=2] {'expert_1'}, use_global_device_ids=true, to_apply=%region_4.0 | all-reduce | flops 256 | bytes 2048 | tf_op jit(solution)/shard_map/pmax | solution.py:17
  28.5 3.8 %pmax.37 = f32[256]{0:T(256)S(1)} all-reduce(f32[256]{0:T(256)S(1)} %pmax.36), channel_id=1, replica_groups=mesh['expert_0'=4,'expert_1'=8,'seq_0'=2,'seq_1'=2,'fsdp'=2] {'seq_0'}, use_global_device_ids=true, to_apply=%region_5.0 | all-reduce | flops 256 | bytes 2048 | tf_op jit(solution)/shard_map/pmax | solution.py:17
  32.3 9.7 %pmax.38 = f32[256]{0:T(256)S(1)} all-reduce(f32[256]{0:T(256)S(1)} %pmax.37), channel_id=1, replica_groups=mesh['expert_0'=4,'expert_1'=8,'seq_0'=2,'seq_1'=2,'fsdp'=2] {'seq_1'}, use_global_device_ids=true, to_apply=%region_6.0 | all-reduce | flops 256 | bytes 2048 | tf_op jit(solution)/shard_map/pmax | solution.py:17
  42.0 5.3 %pmax.39 = f32[256]{0:T(256)S(1)} all-reduce(f32[256]{0:T(256)S(1)} %pmax.38), channel_id=1, replica_groups=mesh['expert_0'=4,'expert_1'=8,'seq_0'=2,'seq_1'=2,'fsdp'=2] {'fsdp'}, use_global_device_ids=true, to_apply=%region_7.0 | all-reduce | flops 256 | bytes 2048 | tf_op jit(solution)/shard_map/pmax | solution.py:17
  47.3 3.6 %convolution_bitcast_fusion = f32[32,8,1280]{2,1,0:T(8,128)} fusion(f32[224,1280]{1,0:T(8,128)} %param.4, f32[224,256]{1,0:T(8,128)S(1)} %get-tuple-element.12, f32[256]{0:T(256)S(1)} %pmax.39), kind=kOutput, calls=%fused_computation | convolution fusion | flops 880861184 | bytes 2688000 | tf_op jit(solution)/shard_map/dot_general | solution.py:75
  50.8 0.8 fusion.3
  51.6 0.9 concatenate.15
  52.5 1.5 pad_maximum_fusion
  54.0 37.3 %all_to_all.21 = f32[32,8,1281]{2,1,0:T(8,128)} all-to-all(f32[32,8,1281]{2,1,0:T(8,128)S(1)} %pad_maximum_fusion), channel_id=1, replica_groups=mesh['expert_0'=4,'expert_1'=8,'seq_0'=2,'seq_1'=2,'fsdp'=2] {'expert_0'..., dimensions={0} | all-to-all | bytes 2623488 | tf_op jit(solution)/shard_map/all_to_all | solution.py:28
  91.3 1.4 reduce_sum.47
  92.7 0.7 slice_reduce_fusion
  93.4 0.6 slice.22
  94.0 0.8 reshape.41
  94.8 0.7 pad_maximum_fusion.1
  95.5 0.2 broadcast_in_dim.6
  95.7 16.7 %all_to_all.22 = f32[8,1,10248]{2,1,0:T(1,128)} all-to-all(f32[8,1,10248]{2,1,0:T(1,128)S(1)} %broadcast_in_dim.6), channel_id=1, replica_groups=mesh['expert_0'=4,'expert_1'=8,'seq_0'=2,'seq_1'=2,'fsdp'=2] {'seq_0','s..., dimensions={0} | all-to-all | bytes 655872 | tf_op jit(solution)/shard_map/all_to_all | solution.py:45
  112.4 1.2 reduce_sum.48
  113.6 0.6 slice.25
  114.2 0.6 slice.24
  114.9 0.8 reshape.43
  115.6 1.3 div.21
  117.0 4.7 %fusion.97 = (u8[4,320]{1,0:T(4,128)(4,1)S(1)}, u8[4,320]{1,0:T(4,128)(4,1)S(1)}, u8[4,320]{1,0:T(4,128)(4,1)S(1)}, f32[2,4,320]{2,1,0:T(4,128)S(1)}) fusion(f32[2,320,1280]{2,1,0:T(8,128)} %param.6, f32[2,4,1280]{2,1,0:T(4,128)S(1)} %reshape.43, f32[2,4]{1,0:T(2,128)} %div.21), kind=kOutput, calls=%fused_computation.114 | convolution fusion | flops 39379200 | bytes 3331872 | tf_op jit(solution)/shard_map/esd,ehd->esh/dot_general | solution.py:99
  121.8 2.3 %fusion.14 = f32[2,4,1280]{2,1,0:T(4,128)} fusion(f32[2,320,1280]{2,1,0:T(8,128)S(1)} %copy-done, pred[2,4,320]{2,1,0:T(4,128)(4,1)S(1)} %and_convert_fusion.2, pred[2,4,320]{2,1,0:T(4,128)(4,1)S(1)} %get-tuple-element.15, pred[2,4,320]{2,1,0:T(4,128)(4,1)S(1)} %get-tuple-element.14, f32[2,4,320]{2,1,0:T(4,128)S(1)} %get-tuple-element.13), kind=kOutput, calls=%fused_computation.21 | convolution fusion | flops 39477760 | bytes 3335680 | tf_op jit(solution)/shard_map/esh,ehd->esd/dot_general | solution.py:101
  124.1 0.8 reshape.44
  124.9 11.0 %all_to_all.23 = f32[8,8,1280]{2,1,0:T(8,128)} all-to-all(f32[8,8,1280]{2,1,0:T(8,128)S(1)} %broadcast_in_dim.14), channel_id=1, replica_groups=mesh['expert_0'=4,'expert_1'=8,'seq_0'=2,'seq_1'=2,'fsdp'=2] {'seq_0','s..., dimensions={0} | all-to-all | bytes 655360 | tf_op jit(solution)/shard_map/all_to_all | solution.py:45
  135.9 1.0 reduce_sum.49
  136.9 0.1 broadcast_in_dim.15
  137.0 0.0 copy-start.1
  137.1 37.3 %all_to_all.24 = f32[32,8,1280]{2,1,0:T(8,128)S(1)} all-to-all(f32[32,8,1280]{2,1,0:T(8,128)S(1)} %broadcast_in_dim.15), channel_id=1, replica_groups=mesh['expert_0'=4,'expert_1'=8,'seq_0'=2,'seq_1'=2,'fsdp'=2] {'expert_0'..., dimensions={0} | all-to-all | bytes 2621440 | tf_op jit(solution)/shard_map/all_to_all | solution.py:45
  174.3 2.1 %fusion = f32[224,1280]{1,0:T(8,128)} fusion(f32[32,8,1280]{2,1,0:T(8,128)S(1)} %all_to_all.24, f32[224,256]{1,0:T(8,128)S(1)} %get-tuple-element.12, f32[224]{0:T(256)S(1)} %copy-done.1, f32[224]{0:T(256)S(1)} %get-tuple-element.7), kind=kOutput, calls=%fused_computation.2 | convolution fusion | flops 880918528 | bytes 2688768 | tf_op jit(solution)/shard_map/dot_general | solution.py:103
  (6 shorter events, 0.1 us)
Async XLA Ops:
  0.0 121.8 %copy-start = (f32[2,320,1280]{2,1,0:T(8,128)S(1)}, f32[2,320,1280]{2,1,0:T(8,128)}, u32[]{:S(2)}) copy-start(f32[2,320,1280]{2,1,0:T(8,128)} %param.7) | copy-start | bytes 9830404
  137.0 37.3 %copy-start.1 = (f32[224]{0:T(256)S(1)}, f32[224]{0:T(256)}, u32[]{:S(2)}) copy-start(f32[224]{0:T(256)} %get-tuple-element.5) | copy-start | bytes 2692
where the time goes:
time: 178 us; the launch traced here: 176 us
  blocking collectives  147 us (83%)
  matrix products  15.8 us (9%)
  local copies, waits for them, and re-layouts  7.38 us (4%)
  other arithmetic  6.63 us (4%)
    all_to_all x3, blocking collectives, sent_to_all(): return lax.all_to_all(copies, axis, split_axis=0, concat_axis=0, tiled=True)  65 us
    pmax x5, blocking collectives, one_axis_at_a_time(): return functools.reduce(lax.pmax, axes, array)  44.2 us
    all_to_all x1, blocking collectives, summed_on_arrival(): lax.all_to_all(in_blocks(array, dim, devices), axis, 0, 0, tiled=True)  37.3 us
    dot_general x1, matrix products, body(): jnp.einsum('esd,ehd->esh', slot_inputs, w_in, precision=highest)  4.74 us
    dot_general x1, matrix products, slot_terms(): lax.dot_general(weights, tokens, (((0,), (0,)), ((), ())), precision=lax....  3.58 us

commit v1 on v0

v1 whole, which is shorter than its diff:
```python
import functools

import jax
import jax.numpy as jnp
from jax import lax
from jax.experimental import pallas as pl
from jax.experimental.pallas import tpu as pltpu
from jax.sharding import Mesh
from jax.sharding import PartitionSpec as P

AXES = ("x", "z", "y_lo", "core", "y_hi")
F32 = jnp.float32
BF16 = jnp.bfloat16
SLOTS = 4
HALF = 640
WIDE = HALF + 128


def split(a):
    hi = a.astype(BF16)
    return hi, (a - hi.astype(F32)).astype(BF16)


def dot(a, b, dims=(((1,), (0,)), ((), ()))):
    return lax.dot_general(a, b, dims, preferred_element_type=F32)


def dot3(ah, al, bh, bl, dims=(((1,), (0,)), ((), ()))):
    return dot(ah, bh, dims) + (dot(ah, bl, dims) + dot(al, bh, dims))


def peak_or_mass(peak, mass, rows):
    lane = lax.broadcasted_iota(jnp.int32, (rows, 128), 1)
    return jnp.where(lane < 64, peak, mass)


def merged(parts):
    peaks = [p[:, HALF : HALF + 1] for p in parts]
    peak = functools.reduce(jnp.maximum, peaks)
    total = None
    for part, own in zip(parts, peaks):
        scaled = part * jnp.exp(own - peak)
        total = scaled if total is None else total + scaled
    rows = total.shape[0]
    return total[:, :HALF], peak_or_mass(peak, total[:, HALF + 64 : HALF + 65], rows)


def layer_kernel(
    NX, NY, NZ, stop,
    tok_hbm, par_hbm, win_hbm, wout_hbm, out_ref,
    tok, par, win, wout, xh, xl, wih, wil, woh, wol,
    tmp, ext, wth, wtl, ch, cl, sums, recv_c, kept,
    recv_a, recv_b, two_a, two_b, recv_a2, recv_b2, zsend, zrecv, inputs, osend, orecv, zout, full,
    ld, sc, rc, s1, r1, s2, r2, s3, r3, s4, r4, s5, r5, s6, r6, s7, r7, s8, r8, s9, r9,
):
    x, z, y_lo, c, y_hi = (lax.axis_index(a) for a in AXES)
    y = y_hi * 2 + y_lo
    tokens, width = tok.shape
    K = 2 * NY
    NXZ = NX * NZ

    def device(dx=0, dy=0, dz=0, dc=0):
        to_y = lax.rem(y + dy, NY)
        return (
            lax.rem(x + dx, NX), lax.rem(z + dz, NZ), lax.rem(to_y, 2),
            lax.rem(c + dc, 2), lax.div(to_y, 2),
        )

    def remote(src, dst, send, recv, **to):
        return pltpu.make_async_remote_copy(
            src_ref=src, dst_ref=dst, send_sem=send, recv_sem=recv,
            device_id=device(**to), device_id_type=pl.DeviceIdType.MESH,
        )

    def put(a):
        for b in range(tmp.shape[0]):
            tmp[b] = a[:, 128 * b : 128 * (b + 1)]

    def every_kth(k):
        return jnp.concatenate([tmp[b, pl.ds(k, NXZ, stride=K), :] for b in range(tmp.shape[0])], axis=1)

    xs, ys, zs = (
        sorted(range(1, n), key=lambda d: -min(d, n - d)) for n in (NX, NY, NZ)
    )
    column = [(dy, dc) for dy in [*ys, 0] for dc in (1, 0) if (dy, dc) != (0, 0)]

    barrier = pltpu.get_barrier_semaphore()
    peers = [dict(dx=d) for d in xs] + [dict(dz=d) for d in zs] + [dict(dy=d, dc=e) for d, e in column]
    for to in peers:
        pl.semaphore_signal(barrier, inc=1, device_id=device(**to), device_id_type=pl.DeviceIdType.MESH)

    steps = width // 256
    loads = []
    for i in range(steps):
        at = pl.ds(256 * i, 256)
        loads.append(pltpu.make_async_copy(tok_hbm.at[:, at], tok.at[:, at], ld.at[2 * i]))
        loads.append(pltpu.make_async_copy(par_hbm.at[at, :], par.at[at, :], ld.at[2 * i + 1]))
    load_win = pltpu.make_async_copy(win_hbm, win, ld.at[2 * steps])
    load_wout = pltpu.make_async_copy(wout_hbm, wout, ld.at[2 * steps + 1])
    for copy in [*loads, load_win, load_wout]:
        copy.start()

    n_slots = par.shape[1]
    pad = xh.shape[0] - tokens
    logits = jnp.zeros((tokens, n_slots), F32)
    for i in range(steps):
        loads[2 * i].wait()
        loads[2 * i + 1].wait()
        at = slice(256 * i, 256 * (i + 1))
        a_hi, a_lo = split(tok[:, at])
        b_hi, b_lo = split(par[at, :])
        xh[0:tokens, at] = a_hi
        xl[0:tokens, at] = a_lo
        logits += dot3(a_hi, a_lo, b_hi, b_lo)
    xh[tokens:, :] = jnp.zeros((pad, width), BF16)
    xl[tokens:, :] = jnp.zeros((pad, width), BF16)

    by_slot = jnp.concatenate([logits, jnp.zeros((pad, n_slots), F32)], axis=0).T
    lane = lax.broadcasted_iota(jnp.int32, by_slot.shape, 1)
    held = lane < tokens
    by_slot = jnp.where(held, by_slot, -3e38)
    peak = jnp.max(by_slot, axis=1, keepdims=True)
    weights = jnp.where(held, jnp.exp(by_slot - peak), 0.0)
    put(weights)
    ext[...] = peak_or_mass(peak, jnp.sum(weights, axis=1, keepdims=True), n_slots)
    for k in range(K):
        row = (k % 2) * (NY * NXZ) + (k // 2) * NXZ
        hi, lo = split(every_kth(k))
        wth[row : row + NXZ, :] = hi
        wtl[row : row + NXZ, :] = lo
        block = ext[pl.ds(k, NXZ, stride=K), :].reshape(NX, NZ, 128)
        for p in range(2):
            sums[p, k % 2, k // 2, :, :, HALF:] = block

    pl.semaphore_wait(barrier, len(peers))
    sends = []
    other = 1 - c
    for p in range(2):
        at = slice(HALF * p, HALF * (p + 1))
        part = dot3(wth[...], wtl[...], xh[:, at], xl[:, at])
        sums[p, :, :, :, :, :HALF] = part.reshape(2, NY, NX, NZ, HALF)
        sends.append(remote(sums.at[p, other], recv_c.at[p], sc.at[p], rc.at[p], dc=1))
        sends[-1].start()

    def fill_weights():
        load_win.wait()
        load_wout.wait()
        wih[...], wil[...] = split(win[...])
        woh[...], wol[...] = split(wout[...])

    def fill_combine():
        row_exp = jnp.exp(logits - jnp.max(logits, axis=1, keepdims=True))
        combine = row_exp / jnp.sum(row_exp, axis=1, keepdims=True)
        put(jnp.concatenate([combine, jnp.zeros((pad, n_slots), F32)], axis=0).T)
        order = [every_kth(2 * b + a) for a in range(2) for b in range(NY)]
        ch[...], cl[...] = split(jnp.concatenate(order, axis=0).T[:tokens])

    def joined(p, yi, xi):
        return merged([sums[p, c, yi, xi], recv_c[p, yi, xi]])

    sends[0].wait_recv()
    stage1 = []
    for i, dy in enumerate([*ys, 0]):
        to = lax.rem(y + dy, NY)
        for xi in range(NX):
            kept[0, to, xi, :, :HALF], kept[0, to, xi, :, HALF:] = joined(0, to, xi)
        if dy:
            stage1.append(remote(kept.at[0, to], recv_a.at[dy - 1], s1.at[dy - 1], r1.at[dy - 1], dy=dy))
            stage1[-1].start()
    sends[1].wait_recv()
    for i, dx in enumerate([*xs, 0]):
        to = lax.rem(x + dx, NX)
        for yi in range(NY):
            kept[1, yi, to, :, :HALF], kept[1, yi, to, :, HALF:] = joined(1, yi, to)
        if dx:
            stage1.append(remote(kept.at[1, :, to], recv_b.at[dx - 1], s2.at[dx - 1], r2.at[dx - 1], dx=dx))
            stage1[-1].start()
    fill_weights()

    for copy in stage1[: len(ys)]:
        copy.wait_recv()
    stage2 = []
    for dx in [*xs, 0]:
        to = lax.rem(x + dx, NX)
        two_a[to, :, :HALF], two_a[to, :, HALF:] = merged([kept[0, y, to]] + [recv_a[d, to] for d in range(NY - 1)])
        if dx:
            stage2.append(remote(two_a.at[to], recv_a2.at[dx - 1], s3.at[dx - 1], r3.at[dx - 1], dx=dx))
            stage2[-1].start()
    for copy in stage1[len(ys) :]:
        copy.wait_recv()
    for dy in [*ys, 0]:
        to = lax.rem(y + dy, NY)
        two_b[to, :, :HALF], two_b[to, :, HALF:] = merged([kept[1, to, x]] + [recv_b[d, to] for d in range(NX - 1)])
        if dy:
            stage2.append(remote(two_b.at[to], recv_b2.at[dy - 1], s4.at[dy - 1], r4.at[dy - 1], dy=dy))
            stage2[-1].start()
    fill_combine()

    for copy in stage2:
        copy.wait_recv()
    rows_a = jnp.concatenate(merged([two_a[x]] + [recv_a2[d] for d in range(NX - 1)]), axis=1)
    rows_b = jnp.concatenate(merged([two_b[y]] + [recv_b2[d] for d in range(NY - 1)]), axis=1)
    for i in range(NZ):
        zsend[i, :, :WIDE] = rows_a[i : i + 1]
        zsend[i, :, WIDE:] = rows_b[i : i + 1]
    stage3 = []
    for dz in zs:
        to = lax.rem(z + dz, NZ)
        stage3.append(remote(zsend.at[to], zrecv.at[dz], s5.at[dz - 1], r5.at[dz - 1], dz=dz))
        stage3[-1].start()
    zrecv[0] = zsend[z]
    for copy in stage3:
        copy.wait_recv()
    k = y * 2 + c
    got = zrecv[...].reshape(NZ, 2 * WIDE)
    for p in range(2):
        part = got[:, WIDE * p : WIDE * (p + 1)]
        own = part[:, HALF : HALF + 1]
        total = jnp.sum(part * jnp.exp(own - jnp.max(own, axis=0, keepdims=True)), axis=0, keepdims=True)
        inputs[k, :, HALF * p : HALF * (p + 1)] = total[:, :HALF] / total[:, HALF + 64 : HALF + 65]

    stage4 = []
    for i, (dy, dc) in enumerate(column):
        stage4.append(remote(inputs.at[k], inputs.at[k], s6.at[i], r6.at[i], dy=dy, dc=dc))
        stage4[-1].start()
    for copy in stage4:
        copy.wait_recv()
    s_hi, s_lo = split(inputs[...].reshape(K, width))
    for e in range(K // SLOTS):
        rows = slice(SLOTS * e, SLOTS * (e + 1))
        v = dot3(s_hi[rows], s_lo[rows], wih[e], wil[e], (((1,), (1,)), ((), ())))
        hidden = v * (1.0 + lax.erf(v * 0.7071067811865476)) * 0.5
        h_hi, h_lo = split(hidden)
        partial = dot3(h_hi, h_lo, woh[e], wol[e])
        for i in range(SLOTS):
            osend[SLOTS * e + i] = partial[i : i + 1]
    stage5 = []
    for i, (dy, dc) in enumerate(column):
        to = lax.rem(y + dy, NY) * 2 + lax.rem(c + dc, 2)
        stage5.append(remote(osend.at[to], orecv.at[i], s7.at[i], r7.at[i], dy=dy, dc=dc))
        stage5[-1].start()
    for copy in stage5:
        copy.wait_recv()
    total = osend[k]
    for i in range(len(column)):
        total += orecv[i]
    zout[z] = total

    stage6 = []
    for dz in zs:
        stage6.append(remote(zout.at[z], zout.at[z], s8.at[dz - 1], r8.at[dz - 1], dz=dz))
        stage6[-1].start()
    for copy in stage6:
        copy.wait_recv()
    rows = zout[...].reshape(NZ, width)
    full[0, c, y, x] = rows[:, :HALF]
    full[1, c, y, x] = rows[:, HALF:]
    stage7 = []
    n = 0

    def spread(ref, **to):
        nonlocal n
        copy = remote(ref, ref, s9.at[n], r9.at[n], **to)
        copy.start()
        n += 1
        return copy

    first_a = [spread(full.at[0, c, y, x], dx=d) for d in xs]
    first_b = [spread(full.at[1, c, y, x], dy=d) for d in ys]
    for copy in first_a:
        copy.wait_recv()
    second_a = [spread(full.at[0, c, y], dy=d) for d in ys]
    for copy in first_b:
        copy.wait_recv()
    second_b = [spread(full.at[1, c, :, x], dx=d) for d in xs]
    third = [spread(full.at[0, c, y], dc=1), spread(full.at[1, c, :, x], dc=1)]
    for d, copy in zip(ys, second_a):
        copy.wait_recv()
        third.append(spread(full.at[0, c, lax.rem(y + NY - d, NY)], dc=1))
    for d, copy in zip(xs, second_b):
        copy.wait_recv()
        third.append(spread(full.at[1, c, :, lax.rem(x + NX - d, NX)], dc=1))
    for copy in third:
        copy.wait_recv()
    for p in range(2):
        f_hi, f_lo = split(full[p].reshape(n_slots, HALF))
        out_ref[:, HALF * p : HALF * (p + 1)] = dot3(ch[...], cl[...], f_hi, f_lo)
    for group in (sends, stage1, stage2, stage3, stage4, stage5, stage6, first_a, first_b, second_a, second_b, third):
        for copy in group:
            copy.wait_send()


def body(NX, NY, NZ, stop, tokens, slot_params, w_in, w_out):
    T, D = tokens.shape
    n_slots = slot_params.shape[1]
    E, H, _ = w_in.shape
    K = 2 * NY
    padded = -(-T // 128) * 128
    anywhere = pl.BlockSpec(memory_space=pl.ANY)
    vmem = pltpu.VMEM
    dma = pltpu.SemaphoreType.DMA
    scratch = [
        vmem((T, D), F32), vmem((D, n_slots), F32), vmem((E, H, D), F32), vmem((E, H, D), F32),
        vmem((padded, D), BF16), vmem((padded, D), BF16),
        vmem((E, H, D), BF16), vmem((E, H, D), BF16), vmem((E, H, D), BF16), vmem((E, H, D), BF16),
        vmem((padded // 128, n_slots, 128), F32), vmem((n_slots, 128), F32),
        vmem((n_slots, padded), BF16), vmem((n_slots, padded), BF16),
        vmem((T, n_slots), BF16), vmem((T, n_slots), BF16),
        vmem((2, 2, NY, NX, NZ, WIDE), F32), vmem((2, NY, NX, NZ, WIDE), F32), vmem((2, NY, NX, NZ, WIDE), F32),
        vmem((NY - 1, NX, NZ, WIDE), F32), vmem((NX - 1, NY, NZ, WIDE), F32),
        vmem((NX, NZ, WIDE), F32), vmem((NY, NZ, WIDE), F32),
        vmem((NX - 1, NZ, WIDE), F32), vmem((NY - 1, NZ, WIDE), F32),
        vmem((NZ, 1, 2 * WIDE), F32), vmem((NZ, 1, 2 * WIDE), F32),
        vmem((K, 1, D), F32), vmem((K, 1, D), F32), vmem((K - 1, 1, D), F32), vmem((NZ, 1, D), F32),
        vmem((2, 2, NY, NX, NZ, HALF), F32),
    ]
    spreads = 2 * (NX - 1) + 2 * (NY - 1) + NX + NY
    counts = (2, NY - 1, NX - 1, NX - 1, NY - 1, NZ - 1, K - 1, K - 1, NZ - 1, spreads)
    scratch.append(dma((2 * (D // 256) + 2,)))
    for count in counts:
        scratch += [dma((count,)), dma((count,))]
    return pl.pallas_call(
        functools.partial(layer_kernel, NX, NY, NZ, stop),
        out_shape=jax.ShapeDtypeStruct((T, D), F32),
        in_specs=[anywhere] * 4,
        out_specs=pl.BlockSpec(memory_space=pltpu.VMEM),
        scratch_shapes=scratch,
        compiler_params=pltpu.CompilerParams(
            collective_id=0, has_side_effects=True, vmem_limit_bytes=60 * 1024 * 1024
        ),
    )(tokens, slot_params, w_in, w_out)


def solution(mesh, NX=4, NY=4, NZ=8, stop=99):
    torus = Mesh(mesh.devices.reshape(NX, NZ, NY // 2, 2, mesh.shape["fsdp"]), AXES)
    every = ("x", "z", "y_lo", "core", "y_hi")
    return jax.shard_map(
        functools.partial(body, NX, NY, NZ, stop),
        mesh=torus,
        in_specs=(
            P(every, None),
            P(),
            P(("x", "z"), ("y_lo", "core", "y_hi"), None),
            P(("x", "z"), ("y_lo", "core", "y_hi"), None),
        ),
        out_specs=P(every, None),
        check_vma=False,
    )
```

time: 178 us -> 60.2 us (0.34)
  blocking collectives: 147 us -> 0 us
  Pallas kernels: 0 us -> 57.8 us
  matrix products: 15.8 us -> 0 us
  other arithmetic: 6.63 us -> 0 us
  local copies, waits for them, and re-layouts: 7.38 us -> 2.34 us
    all_to_all x4 -> x0, blocking collectives: 102 us -> none  [the longest x3 65 us: sent_to_all(): return lax.all_to_all(copies, axis, split_axis=0, concat_axis=0, tiled=True)]
    pallas_call x0 -> x1, Pallas kernels: none -> 57.8 us  [body(): pl.pallas_call(functools.partial(layer_kernel, NX, NY, NZ, stop), out_sha...]
    pmax x5 -> x0, blocking collectives: 44.2 us -> none  [one_axis_at_a_time(): return functools.reduce(lax.pmax, axes, array)]
    dot_general x5 -> x0, matrix products: 15.8 us -> none  [the longest x1 4.74 us: body(): jnp.einsum('esd,ehd->esh', slot_inputs, w_in, precision=highest)]
    reduce_sum x4 -> x0, other arithmetic: 4.43 us -> none  [the longest x2 2.22 us: over_copies(): return jnp.sum(everything, axis=0)]
    slice x4 -> x0, local copies, waits for them, and re-layouts: 2.54 us -> none  [the longest x2 1.33 us: side_by_side(): section = whole[..., at:at + column.shape[along]]]
    reshape x3 -> x0, local copies, waits for them, and re-layouts: 2.37 us -> none  [the longest x1 0.79 us: packed_total(): total[b:e].reshape(a.shape)]
    unnamed x4 -> x1, local copies, waits for them, and re-layouts: 0.01 us -> 2.34 us
where the time goes in v1:
time: 60.2 us; the launch traced here: 60.1 us
  Pallas kernels  57.8 us (96%)
  local copies, waits for them, and re-layouts  2.34 us (4%)
    pallas_call x1, Pallas kernels, body(): pl.pallas_call(functools.partial(layer_kernel, NX, NY, NZ, stop), out_sha...  57.8 us
    unnamed x1, local copies, waits for them, and re-layouts  2.34 us

profile of v1, /device:TPU:1, one launch (start us, length us, event | category | flops | bytes accessed | tf_op | source)
XLA Modules:
  0.0 60.1 jit_solution(8843307909402577209)
XLA Ops:
  0.0 57.8 %shard_map.46 = f32[224,1280]{1,0:T(8,128)} custom-call(f32[224,1280]{1,0:T(8,128)} %tok_hbm.1, f32[1280,256]{1,0:T(8,128)} %par_hbm.1, f32[2,320,1280]{2,1,0:T(8,128)} %win_hbm.1, f32[2,320,1280]{2,1,0:T(8,128)} %wout_hbm.1), custom_call_target="tpu_custom_call" | custom-call | tf_op jit(solution)/shard_map/pallas_call | solution.py:322
  57.8 2.3 %copy.6 = f32[224,1280]{1,0:T(8,128)} copy(f32[224,1280]{1,0:T(8,128)} %shard_map.46) | data formatting | bytes 2293760

commit v2 on v1

--- a/solution.py
+++ b/solution.py
@@ -19,6 +19,9 @@
 def split(a):
     hi = a.astype(BF16)
     return hi, (a - hi.astype(F32)).astype(BF16)
+
+
+TRANSPOSED = (((1,), (1,)), ((), ()))
 
 
 def dot(a, b, dims=(((1,), (0,)), ((), ()))):
@@ -47,10 +50,10 @@
 
 def layer_kernel(
     NX, NY, NZ, stop,
-    tok_hbm, par_hbm, win_hbm, wout_hbm, out_ref,
+    tok_hbm, par_hbm, win_hbm, wout_hbm, full, ch, cl,
     tok, par, win, wout, xh, xl, wih, wil, woh, wol,
-    tmp, ext, wth, wtl, ch, cl, sums, recv_c, kept,
-    recv_a, recv_b, two_a, two_b, recv_a2, recv_b2, zsend, zrecv, inputs, osend, orecv, zout, full,
+    tmp, ext, wth, wtl, sums, recv_c, kept,
+    recv_a, recv_b, two_a, two_b, recv_a2, recv_b2, zsend, zrecv, inputs, osend, orecv, zout,
     ld, sc, rc, s1, r1, s2, r2, s3, r3, s4, r4, s5, r5, s6, r6, s7, r7, s8, r8, s9, r9,
 ):
     x, z, y_lo, c, y_hi = (lax.axis_index(a) for a in AXES)
@@ -145,8 +148,8 @@
     def fill_weights():
         load_win.wait()
         load_wout.wait()
-        wih[...], wil[...] = split(win[...])
-        woh[...], wol[...] = split(wout[...])
+        wih[...], wil[...] = split(win[...].reshape(wih.shape))
+        woh[...], wol[...] = split(wout[...].reshape(woh.shape))
 
     def fill_combine():
         row_exp = jnp.exp(logits - jnp.max(logits, axis=1, keepdims=True))
@@ -155,23 +158,26 @@
         order = [every_kth(2 * b + a) for a in range(2) for b in range(NY)]
         ch[...], cl[...] = split(jnp.concatenate(order, axis=0).T[:tokens])
 
-    def joined(p, yi, xi):
-        return merged([sums[p, c, yi, xi], recv_c[p, yi, xi]])
+    def flat(a):
+        return a.reshape(-1, WIDE)
+
+    def keep(ref, parts):
+        total, block = merged([flat(a) for a in parts])
+        ref[..., :HALF] = total.reshape(*ref.shape[:-1], HALF)
+        ref[..., HALF:] = block.reshape(*ref.shape[:-1], 128)
 
     sends[0].wait_recv()
     stage1 = []
-    for i, dy in enumerate([*ys, 0]):
+    for dy in [*ys, 0]:
         to = lax.rem(y + dy, NY)
-        for xi in range(NX):
-            kept[0, to, xi, :, :HALF], kept[0, to, xi, :, HALF:] = joined(0, to, xi)
+        keep(kept.at[0, to], [sums[0, c, to], recv_c[0, to]])
         if dy:
             stage1.append(remote(kept.at[0, to], recv_a.at[dy - 1], s1.at[dy - 1], r1.at[dy - 1], dy=dy))
             stage1[-1].start()
     sends[1].wait_recv()
-    for i, dx in enumerate([*xs, 0]):
+    for dx in [*xs, 0]:
         to = lax.rem(x + dx, NX)
-        for yi in range(NY):
-            kept[1, yi, to, :, :HALF], kept[1, yi, to, :, HALF:] = joined(1, yi, to)
+        keep(kept.at[1, :, to], [sums[1, c, :, to], recv_c[1, :, to]])
         if dx:
             stage1.append(remote(kept.at[1, :, to], recv_b.at[dx - 1], s2.at[dx - 1], r2.at[dx - 1], dx=dx))
             stage1[-1].start()
@@ -179,21 +185,19 @@
 
     for copy in stage1[: len(ys)]:
         copy.wait_recv()
+    keep(two_a, [kept[0, y]] + [recv_a[d] for d in range(NY - 1)])
     stage2 = []
-    for dx in [*xs, 0]:
+    for dx in xs:
         to = lax.rem(x + dx, NX)
-        two_a[to, :, :HALF], two_a[to, :, HALF:] = merged([kept[0, y, to]] + [recv_a[d, to] for d in range(NY - 1)])
-        if dx:
-            stage2.append(remote(two_a.at[to], recv_a2.at[dx - 1], s3.at[dx - 1], r3.at[dx - 1], dx=dx))
-            stage2[-1].start()
+        stage2.append(remote(two_a.at[to], recv_a2.at[dx - 1], s3.at[dx - 1], r3.at[dx - 1], dx=dx))
+        stage2[-1].start()
     for copy in stage1[len(ys) :]:
         copy.wait_recv()
-    for dy in [*ys, 0]:
+    keep(two_b, [kept[1, :, x]] + [recv_b[d] for d in range(NX - 1)])
+    for dy in ys:
         to = lax.rem(y + dy, NY)
-        two_b[to, :, :HALF], two_b[to, :, HALF:] = merged([kept[1, to, x]] + [recv_b[d, to] for d in range(NX - 1)])
-        if dy:
-            stage2.append(remote(two_b.at[to], recv_b2.at[dy - 1], s4.at[dy - 1], r4.at[dy - 1], dy=dy))
-            stage2[-1].start()
+        stage2.append(remote(two_b.at[to], recv_b2.at[dy - 1], s4.at[dy - 1], r4.at[dy - 1], dy=dy))
+        stage2[-1].start()
     fill_combine()
 
     for copy in stage2:
@@ -226,14 +230,18 @@
     for copy in stage4:
         copy.wait_recv()
     s_hi, s_lo = split(inputs[...].reshape(K, width))
-    for e in range(K // SLOTS):
-        rows = slice(SLOTS * e, SLOTS * (e + 1))
-        v = dot3(s_hi[rows], s_lo[rows], wih[e], wil[e], (((1,), (1,)), ((), ())))
-        hidden = v * (1.0 + lax.erf(v * 0.7071067811865476)) * 0.5
-        h_hi, h_lo = split(hidden)
-        partial = dot3(h_hi, h_lo, woh[e], wol[e])
-        for i in range(SLOTS):
-            osend[SLOTS * e + i] = partial[i : i + 1]
+    units = wih.shape[0]
+    both = dot(jnp.concatenate([s_hi, s_lo], axis=0), wih[...], TRANSPOSED)
+    v = both[:K] + (both[K:] + dot(s_hi, wil[...], TRANSPOSED))
+    slot = lax.broadcasted_iota(jnp.int32, v.shape, 0)
+    unit = lax.broadcasted_iota(jnp.int32, v.shape, 1)
+    own = slot // SLOTS == unit // (units // (K // SLOTS))
+    hidden = jnp.where(own, v * (1.0 + lax.erf(v * 0.7071067811865476)) * 0.5, 0.0)
+    h_hi, h_lo = split(hidden)
+    both = dot(jnp.concatenate([h_hi, h_lo], axis=0), woh[...])
+    partial = both[:K] + (both[K:] + dot(h_hi, wol[...]))
+    for i in range(K):
+        osend[i] = partial[i : i + 1]
     stage5 = []
     for i, (dy, dc) in enumerate(column):
         to = lax.rem(y + dy, NY) * 2 + lax.rem(c + dc, 2)
@@ -282,12 +290,25 @@
         third.append(spread(full.at[1, c, :, lax.rem(x + NX - d, NX)], dc=1))
     for copy in third:
         copy.wait_recv()
-    for p in range(2):
-        f_hi, f_lo = split(full[p].reshape(n_slots, HALF))
-        out_ref[:, HALF * p : HALF * (p + 1)] = dot3(ch[...], cl[...], f_hi, f_lo)
     for group in (sends, stage1, stage2, stage3, stage4, stage5, stage6, first_a, first_b, second_a, second_b, third):
         for copy in group:
             copy.wait_send()
+
+
+def mix_kernel(full, ch, cl, out_hbm, out, sem):
+    copies = []
+    n_slots = ch.shape[1]
+    for p in range(2):
+        f_hi, f_lo = split(full[p].reshape(n_slots, HALF))
+        for start, end in ((0, 256), (256, 512), (512, 640)) if p == 0 else ((0, 128), (128, 384), (384, 640)):
+            at = slice(HALF * p + start, HALF * p + end)
+            out[:, at] = dot3(ch[...], cl[...], f_hi[:, start:end], f_lo[:, start:end])
+            if at.stop % 256 == 0:
+                done = pl.ds(at.stop - 256, 256)
+                copies.append(pltpu.make_async_copy(out.at[:, done], out_hbm.at[:, done], sem.at[len(copies)]))
+                copies[-1].start()
+    for copy in copies:
+        copy.wait()
 
 
 def body(NX, NY, NZ, stop, tokens, slot_params, w_in, w_out):
@@ -296,39 +317,52 @@
     E, H, _ = w_in.shape
     K = 2 * NY
     padded = -(-T // 128) * 128
-    anywhere = pl.BlockSpec(memory_space=pl.ANY)
+    anywhere = pl.BlockSpec(memory_space=pltpu.MemorySpace.HBM)
     vmem = pltpu.VMEM
     dma = pltpu.SemaphoreType.DMA
     scratch = [
         vmem((T, D), F32), vmem((D, n_slots), F32), vmem((E, H, D), F32), vmem((E, H, D), F32),
         vmem((padded, D), BF16), vmem((padded, D), BF16),
-        vmem((E, H, D), BF16), vmem((E, H, D), BF16), vmem((E, H, D), BF16), vmem((E, H, D), BF16),
+        vmem((E * H, D), BF16), vmem((E * H, D), BF16), vmem((E * H, D), BF16), vmem((E * H, D), BF16),
         vmem((padded // 128, n_slots, 128), F32), vmem((n_slots, 128), F32),
         vmem((n_slots, padded), BF16), vmem((n_slots, padded), BF16),
-        vmem((T, n_slots), BF16), vmem((T, n_slots), BF16),
         vmem((2, 2, NY, NX, NZ, WIDE), F32), vmem((2, NY, NX, NZ, WIDE), F32), vmem((2, NY, NX, NZ, WIDE), F32),
         vmem((NY - 1, NX, NZ, WIDE), F32), vmem((NX - 1, NY, NZ, WIDE), F32),
         vmem((NX, NZ, WIDE), F32), vmem((NY, NZ, WIDE), F32),
         vmem((NX - 1, NZ, WIDE), F32), vmem((NY - 1, NZ, WIDE), F32),
         vmem((NZ, 1, 2 * WIDE), F32), vmem((NZ, 1, 2 * WIDE), F32),
         vmem((K, 1, D), F32), vmem((K, 1, D), F32), vmem((K - 1, 1, D), F32), vmem((NZ, 1, D), F32),
-        vmem((2, 2, NY, NX, NZ, HALF), F32),
     ]
     spreads = 2 * (NX - 1) + 2 * (NY - 1) + NX + NY
     counts = (2, NY - 1, NX - 1, NX - 1, NY - 1, NZ - 1, K - 1, K - 1, NZ - 1, spreads)
     scratch.append(dma((2 * (D // 256) + 2,)))
     for count in counts:
         scratch += [dma((count,)), dma((count,))]
-    return pl.pallas_call(
+    args = [pltpu.with_memory_space_constraint(a, pltpu.MemorySpace.HBM) for a in (tokens, slot_params, w_in, w_out)]
+    full, ch, cl = pl.pallas_call(
         functools.partial(layer_kernel, NX, NY, NZ, stop),
-        out_shape=jax.ShapeDtypeStruct((T, D), F32),
+        out_shape=(
+            jax.ShapeDtypeStruct((2, 2, NY, NX, NZ, HALF), F32),
+            jax.ShapeDtypeStruct((T, n_slots), BF16),
+            jax.ShapeDtypeStruct((T, n_slots), BF16),
+        ),
         in_specs=[anywhere] * 4,
-        out_specs=pl.BlockSpec(memory_space=pltpu.VMEM),
+        out_specs=(pl.BlockSpec(memory_space=pltpu.VMEM),) * 3,
         scratch_shapes=scratch,
         compiler_params=pltpu.CompilerParams(
-            collective_id=0, has_side_effects=True, vmem_limit_bytes=60 * 1024 * 1024
+            collective_id=0, has_side_effects=True, vmem_limit_bytes=40 * 1024 * 1024
         ),
-    )(tokens, slot_params, w_in, w_out)
+        name="layer",
+    )(*args)
+    return pl.pallas_call(
+        mix_kernel,
+        out_shape=jax.ShapeDtypeStruct((T, D), F32),
+        in_specs=[pl.BlockSpec(memory_space=pltpu.VMEM)] * 3,
+        out_specs=anywhere,
+        scratch_shapes=[vmem((T, D), F32), dma((D // 256,))],
+        compiler_params=pltpu.CompilerParams(vmem_limit_bytes=16 * 1024 * 1024),
+        name="mix",
+    )(full, ch, cl)
 
 
 def solution(mesh, NX=4, NY=4, NZ=8, stop=99):

time: 60.2 us -> 54.9 us (0.912)
  Pallas kernels: 57.8 us -> 54.8 us
  local copies, waits for them, and re-layouts: 2.34 us -> 0 us
    pallas_call x1, Pallas kernels: 57.8 us -> 53.3 us  [body(): pl.pallas_call(functools.partial(layer_kernel, NX, NY, NZ, stop), out_sha...]
    unnamed x1 -> x0, local copies, waits for them, and re-layouts: 2.34 us -> none
    pallas_call x0 -> x1, Pallas kernels: none -> 1.53 us  [body(): pl.pallas_call(mix_kernel, out_shape=jax.ShapeDtypeStruct((T, D), F32), i...]
where the time goes in v2:
time: 54.9 us; the launch traced here: 54.8 us
  Pallas kernels  54.8 us (100%)
    pallas_call x1, Pallas kernels, body(): pl.pallas_call(functools.partial(layer_kernel, NX, NY, NZ, stop), out_sha...  53.3 us
    pallas_call x1, Pallas kernels, body(): pl.pallas_call(mix_kernel, out_shape=jax.ShapeDtypeStruct((T, D), F32), i...  1.53 us

profile of v2, /device:TPU:1, one launch (start us, length us, event | category | flops | bytes accessed | tf_op | source)
XLA Modules:
  0.0 54.8 jit_solution(1851439753164211182)
XLA Ops:
  0.0 53.3 %layer.1 = (f32[2,2,4,4,8,640]{5,4,3,2,1,0:T(8,128)S(1)}, bf16[224,256]{1,0:T(8,128)(2,1)S(1)}, bf16[224,256]{1,0:T(8,128)(2,1)S(1)}) custom-call(f32[224,1280]{1,0:T(8,128)} %tok_hbm.1, f32[1280,256]{1,0:T(8,128)} %par_hbm.1, f32[2,320,1280]{2,1,0:T(8,128)} %win_hbm.1, f32[2,320,1280]{2,1,0:T(8,128)} %wout_hbm.1), custom_call_target="tpu_custom_call" | custom-call | tf_op jit(solution)/shard_map/layer/pallas_call | solution.py:342
  53.3 1.5 %mix.1 = f32[224,1280]{1,0:T(8,128)} custom-call(f32[2,2,4,4,8,640]{5,4,3,2,1,0:T(8,128)S(1)} %get-tuple-element.8.full, bf16[224,256]{1,0:T(8,128)(2,1)S(1)} %get-tuple-element.9.ch, bf16[224,256]{1,0:T(8,128)(2,1)S(1)} %get-tuple-element.10.cl), custom_call_target="tpu_custom_call" | custom-call | tf_op jit(solution)/shard_map/mix/pallas_call | solution.py:357

commit v3 on v2

--- a/solution.py
+++ b/solution.py
@@ -28,8 +28,8 @@
     return lax.dot_general(a, b, dims, preferred_element_type=F32)
 
 
-def dot3(ah, al, bh, bl, dims=(((1,), (0,)), ((), ()))):
-    return dot(ah, bh, dims) + (dot(ah, bl, dims) + dot(al, bh, dims))
+def dot3(ah, al, bh, bl):
+    return dot(ah, bh) + (dot(ah, bl) + dot(al, bh))
 
 
 def peak_or_mass(peak, mass, rows):
@@ -53,8 +53,8 @@
     tok_hbm, par_hbm, win_hbm, wout_hbm, full, ch, cl,
     tok, par, win, wout, xh, xl, wih, wil, woh, wol,
     tmp, ext, wth, wtl, sums, recv_c, kept,
-    recv_a, recv_b, two_a, two_b, recv_a2, recv_b2, zsend, zrecv, inputs, osend, orecv, zout,
-    ld, sc, rc, s1, r1, s2, r2, s3, r3, s4, r4, s5, r5, s6, r6, s7, r7, s8, r8, s9, r9,
+    recv_a, recv_b, rows_a, rows_b, got_a, got_b, inputs, osend, orecv, own_out, all_a, all_b,
+    ld, sent, came,
 ):
     x, z, y_lo, c, y_hi = (lax.axis_index(a) for a in AXES)
     y = y_hi * 2 + y_lo
@@ -69,9 +69,9 @@
             lax.rem(c + dc, 2), lax.div(to_y, 2),
         )
 
-    def remote(src, dst, send, recv, **to):
+    def remote(src, dst, group, arrival=None, **to):
         return pltpu.make_async_remote_copy(
-            src_ref=src, dst_ref=dst, send_sem=send, recv_sem=recv,
+            src_ref=src, dst_ref=dst, send_sem=sent.at[group], recv_sem=came.at[group if arrival is None else arrival],
             device_id=device(**to), device_id_type=pl.DeviceIdType.MESH,
         )
 
@@ -82,15 +82,25 @@
     def every_kth(k):
         return jnp.concatenate([tmp[b, pl.ds(k, NXZ, stride=K), :] for b in range(tmp.shape[0])], axis=1)
 
-    xs, ys, zs = (
-        sorted(range(1, n), key=lambda d: -min(d, n - d)) for n in (NX, NY, NZ)
+    def hops(d, n):
+        return min(d, n - d)
+
+    xs, ys = (sorted(range(1, n), key=lambda d: -hops(d, n)) for n in (NX, NY))
+    whole = []
+
+    def one_wait(group, ref):
+        copy = remote(ref, ref, group, dc=1)
+        copy.wait_recv()
+        whole.append(copy)
+
+    column = [(dy, dc) for dy in [*ys, 0] for dc in (1, 0) if (dy, dc) != (0, 0)]
+    plane_a, plane_b = (
+        sorted(
+            ((d, dz) for d in range(n) for dz in range(NZ) if (d, dz) != (0, 0)),
+            key=lambda to: -hops(to[0], n) - hops(to[1], NZ),
+        )
+        for n in (NX, NY)
     )
-    column = [(dy, dc) for dy in [*ys, 0] for dc in (1, 0) if (dy, dc) != (0, 0)]
-
-    barrier = pltpu.get_barrier_semaphore()
-    peers = [dict(dx=d) for d in xs] + [dict(dz=d) for d in zs] + [dict(dy=d, dc=e) for d, e in column]
-    for to in peers:
-        pl.semaphore_signal(barrier, inc=1, device_id=device(**to), device_id_type=pl.DeviceIdType.MESH)
 
     steps = width // 256
     loads = []
@@ -102,6 +112,11 @@
     load_wout = pltpu.make_async_copy(wout_hbm, wout, ld.at[2 * steps + 1])
     for copy in [*loads, load_win, load_wout]:
         copy.start()
+
+    barrier = pltpu.get_barrier_semaphore()
+    peers = [dict(dc=1)] + [dict(dx=d) for d in xs] + [dict(dy=d) for d in ys] + [dict(dz=d) for d in range(1, NZ)]
+    for to in peers:
+        pl.semaphore_signal(barrier, inc=1, device_id=device(**to), device_id_type=pl.DeviceIdType.MESH)
 
     n_slots = par.shape[1]
     pad = xh.shape[0] - tokens
@@ -135,14 +150,15 @@
         for p in range(2):
             sums[p, k % 2, k // 2, :, :, HALF:] = block
 
-    pl.semaphore_wait(barrier, len(peers))
     sends = []
     other = 1 - c
     for p in range(2):
         at = slice(HALF * p, HALF * (p + 1))
         part = dot3(wth[...], wtl[...], xh[:, at], xl[:, at])
         sums[p, :, :, :, :, :HALF] = part.reshape(2, NY, NX, NZ, HALF)
-        sends.append(remote(sums.at[p, other], recv_c.at[p], sc.at[p], rc.at[p], dc=1))
+        if p == 0:
+            pl.semaphore_wait(barrier, len(peers))
+        sends.append(remote(sums.at[p, other], recv_c.at[p], p, dc=1))
         sends[-1].start()
 
     def fill_weights():
@@ -167,68 +183,47 @@
         ref[..., HALF:] = block.reshape(*ref.shape[:-1], 128)
 
     sends[0].wait_recv()
-    stage1 = []
-    for dy in [*ys, 0]:
+    for dy in ys:
         to = lax.rem(y + dy, NY)
         keep(kept.at[0, to], [sums[0, c, to], recv_c[0, to]])
-        if dy:
-            stage1.append(remote(kept.at[0, to], recv_a.at[dy - 1], s1.at[dy - 1], r1.at[dy - 1], dy=dy))
-            stage1[-1].start()
+        remote(kept.at[0, to], recv_a.at[dy - 1], 2, dy=dy).start()
     sends[1].wait_recv()
-    for dx in [*xs, 0]:
+    for dx in xs:
         to = lax.rem(x + dx, NX)
         keep(kept.at[1, :, to], [sums[1, c, :, to], recv_c[1, :, to]])
-        if dx:
-            stage1.append(remote(kept.at[1, :, to], recv_b.at[dx - 1], s2.at[dx - 1], r2.at[dx - 1], dx=dx))
-            stage1[-1].start()
+        remote(kept.at[1, :, to], recv_b.at[dx - 1], 3, dx=dx).start()
+    keep(kept.at[0, y], [sums[0, c, y], recv_c[0, y]])
+    keep(kept.at[1, :, x], [sums[1, c, :, x], recv_c[1, :, x]])
     fill_weights()
 
-    for copy in stage1[: len(ys)]:
-        copy.wait_recv()
-    keep(two_a, [kept[0, y]] + [recv_a[d] for d in range(NY - 1)])
-    stage2 = []
-    for dx in xs:
-        to = lax.rem(x + dx, NX)
-        stage2.append(remote(two_a.at[to], recv_a2.at[dx - 1], s3.at[dx - 1], r3.at[dx - 1], dx=dx))
-        stage2[-1].start()
-    for copy in stage1[len(ys) :]:
-        copy.wait_recv()
-    keep(two_b, [kept[1, :, x]] + [recv_b[d] for d in range(NX - 1)])
-    for dy in ys:
-        to = lax.rem(y + dy, NY)
-        stage2.append(remote(two_b.at[to], recv_b2.at[dy - 1], s4.at[dy - 1], r4.at[dy - 1], dy=dy))
-        stage2[-1].start()
+    def to_owners(rows, own, received, got, group, plane, n, at, axis):
+        total, block = merged([flat(a) for a in [own, *received]])
+        total = jnp.concatenate([total, block], axis=1)
+        for i in range(n * NZ):
+            rows[i // NZ, i % NZ] = total[i : i + 1]
+        for d, dz in plane:
+            src = rows.at[lax.rem(at + d, n), lax.rem(z + dz, NZ)]
+            remote(src, got.at[d * NZ + dz], group, **{axis: d}, dz=dz).start()
+        got[0] = rows[at, z]
+
+    one_wait(2, recv_a)
+    one_wait(3, recv_b)
+    to_owners(rows_a, kept[0, y], [recv_a[d] for d in range(NY - 1)], got_a, 4, plane_a, NX, x, "dx")
+    to_owners(rows_b, kept[1, :, x], [recv_b[d] for d in range(NX - 1)], got_b, 5, plane_b, NY, y, "dy")
     fill_combine()
 
-    for copy in stage2:
-        copy.wait_recv()
-    rows_a = jnp.concatenate(merged([two_a[x]] + [recv_a2[d] for d in range(NX - 1)]), axis=1)
-    rows_b = jnp.concatenate(merged([two_b[y]] + [recv_b2[d] for d in range(NY - 1)]), axis=1)
-    for i in range(NZ):
-        zsend[i, :, :WIDE] = rows_a[i : i + 1]
-        zsend[i, :, WIDE:] = rows_b[i : i + 1]
-    stage3 = []
-    for dz in zs:
-        to = lax.rem(z + dz, NZ)
-        stage3.append(remote(zsend.at[to], zrecv.at[dz], s5.at[dz - 1], r5.at[dz - 1], dz=dz))
-        stage3[-1].start()
-    zrecv[0] = zsend[z]
-    for copy in stage3:
-        copy.wait_recv()
+    one_wait(4, got_a.at[1:])
+    one_wait(5, got_b.at[1:])
     k = y * 2 + c
-    got = zrecv[...].reshape(NZ, 2 * WIDE)
-    for p in range(2):
-        part = got[:, WIDE * p : WIDE * (p + 1)]
+    for p, got in enumerate((got_a, got_b)):
+        part = got[...].reshape(-1, WIDE)
         own = part[:, HALF : HALF + 1]
         total = jnp.sum(part * jnp.exp(own - jnp.max(own, axis=0, keepdims=True)), axis=0, keepdims=True)
         inputs[k, :, HALF * p : HALF * (p + 1)] = total[:, :HALF] / total[:, HALF + 64 : HALF + 65]
 
-    stage4 = []
-    for i, (dy, dc) in enumerate(column):
-        stage4.append(remote(inputs.at[k], inputs.at[k], s6.at[i], r6.at[i], dy=dy, dc=dc))
-        stage4[-1].start()
-    for copy in stage4:
-        copy.wait_recv()
+    for dy, dc in column:
+        remote(inputs.at[k], inputs.at[k], 6, dy=dy, dc=dc).start()
+    one_wait(6, inputs.at[1:])
     s_hi, s_lo = split(inputs[...].reshape(K, width))
     units = wih.shape[0]
     both = dot(jnp.concatenate([s_hi, s_lo], axis=0), wih[...], TRANSPOSED)
@@ -242,57 +237,57 @@
     partial = both[:K] + (both[K:] + dot(h_hi, wol[...]))
     for i in range(K):
         osend[i] = partial[i : i + 1]
-    stage5 = []
     for i, (dy, dc) in enumerate(column):
         to = lax.rem(y + dy, NY) * 2 + lax.rem(c + dc, 2)
-        stage5.append(remote(osend.at[to], orecv.at[i], s7.at[i], r7.at[i], dy=dy, dc=dc))
-        stage5[-1].start()
-    for copy in stage5:
-        copy.wait_recv()
+        remote(osend.at[to], orecv.at[i], 7, dy=dy, dc=dc).start()
+    one_wait(7, orecv)
     total = osend[k]
     for i in range(len(column)):
         total += orecv[i]
-    zout[z] = total
-
-    stage6 = []
-    for dz in zs:
-        stage6.append(remote(zout.at[z], zout.at[z], s8.at[dz - 1], r8.at[dz - 1], dz=dz))
-        stage6[-1].start()
-    for copy in stage6:
-        copy.wait_recv()
-    rows = zout[...].reshape(NZ, width)
-    full[0, c, y, x] = rows[:, :HALF]
-    full[1, c, y, x] = rows[:, HALF:]
-    stage7 = []
-    n = 0
-
-    def spread(ref, **to):
-        nonlocal n
-        copy = remote(ref, ref, s9.at[n], r9.at[n], **to)
-        copy.start()
-        n += 1
-        return copy
-
-    first_a = [spread(full.at[0, c, y, x], dx=d) for d in xs]
-    first_b = [spread(full.at[1, c, y, x], dy=d) for d in ys]
-    for copy in first_a:
-        copy.wait_recv()
-    second_a = [spread(full.at[0, c, y], dy=d) for d in ys]
-    for copy in first_b:
-        copy.wait_recv()
-    second_b = [spread(full.at[1, c, :, x], dx=d) for d in xs]
-    third = [spread(full.at[0, c, y], dc=1), spread(full.at[1, c, :, x], dc=1)]
-    for d, copy in zip(ys, second_a):
-        copy.wait_recv()
-        third.append(spread(full.at[0, c, lax.rem(y + NY - d, NY)], dc=1))
-    for d, copy in zip(xs, second_b):
-        copy.wait_recv()
-        third.append(spread(full.at[1, c, :, lax.rem(x + NX - d, NX)], dc=1))
-    for copy in third:
-        copy.wait_recv()
-    for group in (sends, stage1, stage2, stage3, stage4, stage5, stage6, first_a, first_b, second_a, second_b, third):
-        for copy in group:
-            copy.wait_send()
+    own_out[0] = total[:, :HALF]
+    own_out[1] = total[:, HALF:]
+
+    def to_plane(src, everything, group, plane, at, axis):
+        row = at * NZ + z
+        for d, dz in plane:
+            remote(src, everything.at[row], group, **{axis: d}, dz=dz).start()
+        everything[row] = src[...]
+
+    to_plane(own_out.at[0], all_a, 8, plane_a, x, "dx")
+    to_plane(own_out.at[1], all_b, 9, plane_b, y, "dy")
+
+    def block(p, d=0):
+        if p == 0:
+            return full.at[0, c, lax.rem(y + NY - d, NY)]
+        return full.at[1, c, :, lax.rem(x + NX - d, NX)]
+
+    def spread(p, ds, axis):
+        copies = {}
+        for d in ds:
+            copies[d] = remote(block(p), block(p), 10 + p, 10 + 3 * p + d, **{axis: d})
+            copies[d].start()
+        remote(block(p), block(p), 12, 17, dc=1).start()
+        return copies
+
+    one_wait(8, all_a.at[1:])
+    full[0, c, y] = all_a[...].reshape(NX, NZ, HALF)
+    last_a = spread(0, ys, "dy")
+    one_wait(9, all_b.at[1:])
+    full[1, c, :, x] = all_b[...].reshape(NY, NZ, HALF)
+    last_b = spread(1, xs, "dx")
+    for d in reversed(ys):
+        last_a[d].wait_recv()
+        remote(block(0, d), block(0, d), 12, 17, dc=1).start()
+    for d in reversed(xs):
+        last_b[d].wait_recv()
+        remote(block(1, d), block(1, d), 12, 17, dc=1).start()
+    theirs = full.at[:, other]
+    remote(theirs, theirs, 12, 17, dc=1).wait()
+    for copy in sends + whole:
+        copy.wait_send()
+    three_a, three_b = full.at[0, c, 1:], full.at[1, c, :, 1:]
+    remote(three_a, three_a, 10, dc=1).wait_send()
+    remote(three_b, three_b, 11, dc=1).wait_send()
 
 
 def mix_kernel(full, ch, cl, out_hbm, out, sem):
@@ -328,16 +323,12 @@
         vmem((n_slots, padded), BF16), vmem((n_slots, padded), BF16),
         vmem((2, 2, NY, NX, NZ, WIDE), F32), vmem((2, NY, NX, NZ, WIDE), F32), vmem((2, NY, NX, NZ, WIDE), F32),
         vmem((NY - 1, NX, NZ, WIDE), F32), vmem((NX - 1, NY, NZ, WIDE), F32),
-        vmem((NX, NZ, WIDE), F32), vmem((NY, NZ, WIDE), F32),
-        vmem((NX - 1, NZ, WIDE), F32), vmem((NY - 1, NZ, WIDE), F32),
-        vmem((NZ, 1, 2 * WIDE), F32), vmem((NZ, 1, 2 * WIDE), F32),
-        vmem((K, 1, D), F32), vmem((K, 1, D), F32), vmem((K - 1, 1, D), F32), vmem((NZ, 1, D), F32),
+        vmem((NX, NZ, 1, WIDE), F32), vmem((NY, NZ, 1, WIDE), F32),
+        vmem((NX * NZ, 1, WIDE), F32), vmem((NY * NZ, 1, WIDE), F32),
+        vmem((K, 1, D), F32), vmem((K, 1, D), F32), vmem((K - 1, 1, D), F32), vmem((2, 1, HALF), F32),
+        vmem((NX * NZ, 1, HALF), F32), vmem((NY * NZ, 1, HALF), F32),
     ]
-    spreads = 2 * (NX - 1) + 2 * (NY - 1) + NX + NY
-    counts = (2, NY - 1, NX - 1, NX - 1, NY - 1, NZ - 1, K - 1, K - 1, NZ - 1, spreads)
-    scratch.append(dma((2 * (D // 256) + 2,)))
-    for count in counts:
-        scratch += [dma((count,)), dma((count,))]
+    scratch += [dma((2 * (D // 256) + 2,)), dma((13,)), dma((18,))]
     args = [pltpu.with_memory_space_constraint(a, pltpu.MemorySpace.HBM) for a in (tokens, slot_params, w_in, w_out)]
     full, ch, cl = pl.pallas_call(
         functools.partial(layer_kernel, NX, NY, NZ, stop),

time: 54.9 us -> 52.3 us (0.953)
  Pallas kernels: 54.8 us -> 52.2 us
    pallas_call x1, Pallas kernels: 53.3 us -> 50.7 us  [body(): pl.pallas_call(functools.partial(layer_kernel, NX, NY, NZ, stop), out_sha...]
where the time goes in v3:
time: 52.3 us; the launch traced here: 52.2 us
  Pallas kernels  52.2 us (100%)
    pallas_call x1, Pallas kernels, body(): pl.pallas_call(functools.partial(layer_kernel, NX, NY, NZ, stop), out_sha...  50.7 us
    pallas_call x1, Pallas kernels, body(): pl.pallas_call(mix_kernel, out_shape=jax.ShapeDtypeStruct((T, D), F32), i...  1.53 us

profile of v3, /device:TPU:1, one launch (start us, length us, event | category | flops | bytes accessed | tf_op | source)
XLA Modules:
  0.0 52.2 jit_solution(13053080252199573170)
XLA Ops:
  0.0 50.7 %layer.1 = (f32[2,2,4,4,8,640]{5,4,3,2,1,0:T(8,128)S(1)}, bf16[224,256]{1,0:T(8,128)(2,1)S(1)}, bf16[224,256]{1,0:T(8,128)(2,1)S(1)}) custom-call(f32[224,1280]{1,0:T(8,128)} %tok_hbm.1, f32[1280,256]{1,0:T(8,128)} %par_hbm.1, f32[2,320,1280]{2,1,0:T(8,128)} %win_hbm.1, f32[2,320,1280]{2,1,0:T(8,128)} %wout_hbm.1), custom_call_target="tpu_custom_call" | custom-call | tf_op jit(solution)/shard_map/layer/pallas_call | solution.py:333
  50.7 1.5 %mix.1 = f32[224,1280]{1,0:T(8,128)} custom-call(f32[2,2,4,4,8,640]{5,4,3,2,1,0:T(8,128)S(1)} %get-tuple-element.8.full, bf16[224,256]{1,0:T(8,128)(2,1)S(1)} %get-tuple-element.9.ch, bf16[224,256]{1,0:T(8,128)(2,1)S(1)} %get-tuple-element.10.cl), custom_call_target="tpu_custom_call" | custom-call | tf_op jit(solution)/shard_map/mix/pallas_call | solution.py:348

commit v4 on v3

--- a/solution.py
+++ b/solution.py
@@ -13,6 +13,7 @@
 BF16 = jnp.bfloat16
 SLOTS = 4
 HALF = 640
+FIRST = 768
 WIDE = HALF + 128
 
 
@@ -21,11 +22,8 @@
     return hi, (a - hi.astype(F32)).astype(BF16)
 
 
-TRANSPOSED = (((1,), (1,)), ((), ()))
-
-
-def dot(a, b, dims=(((1,), (0,)), ((), ()))):
-    return lax.dot_general(a, b, dims, preferred_element_type=F32)
+def dot(a, b):
+    return jnp.dot(a, b, preferred_element_type=F32)
 
 
 def dot3(ah, al, bh, bl):
@@ -37,23 +35,28 @@
     return jnp.where(lane < 64, peak, mass)
 
 
+def unpacked(a):
+    return a[:, :HALF], a[:, HALF : HALF + 1], a[:, HALF + 64 : HALF + 65]
+
+
 def merged(parts):
-    peaks = [p[:, HALF : HALF + 1] for p in parts]
-    peak = functools.reduce(jnp.maximum, peaks)
-    total = None
-    for part, own in zip(parts, peaks):
-        scaled = part * jnp.exp(own - peak)
-        total = scaled if total is None else total + scaled
-    rows = total.shape[0]
-    return total[:, :HALF], peak_or_mass(peak, total[:, HALF + 64 : HALF + 65], rows)
+    top = functools.reduce(jnp.maximum, [peak for _, peak, _ in parts])
+    scales = [jnp.exp(peak - top) for _, peak, _ in parts]
+    total = sum(part * scale for (part, _, _), scale in zip(parts, scales))
+    return total, top, sum(mass * scale for (_, _, mass), scale in zip(parts, scales))
+
+
+def group_lanes(groups, rows):
+    lane = lax.broadcasted_iota(jnp.int32, (rows, 128), 1)
+    return lane, 64 // groups
 
 
 def layer_kernel(
     NX, NY, NZ, stop,
-    tok_hbm, par_hbm, win_hbm, wout_hbm, full, ch, cl,
+    tok_hbm, par_hbm, win_hbm, wout_hbm, their_a, their_b, mixed, ch, cl,
     tok, par, win, wout, xh, xl, wih, wil, woh, wol,
-    tmp, ext, wth, wtl, sums, recv_c, kept,
-    recv_a, recv_b, rows_a, rows_b, got_a, got_b, inputs, osend, orecv, own_out, all_a, all_b,
+    tmp, ext, wth, wtl, sums, recv_c, kept, notes_a, notes_b, came_a, came_b,
+    recv_a, recv_b, rows_a, rows_b, got_a, got_b, inputs, osend, orecv, out_a, out_b, all_a, all_b, own_a, own_b, oh, ol,
     ld, sent, came,
 ):
     x, z, y_lo, c, y_hi = (lax.axis_index(a) for a in AXES)
@@ -88,8 +91,8 @@
     xs, ys = (sorted(range(1, n), key=lambda d: -hops(d, n)) for n in (NX, NY))
     whole = []
 
-    def one_wait(group, ref):
-        copy = remote(ref, ref, group, dc=1)
+    def one_wait(group, ref, arrival=None):
+        copy = remote(ref, ref, group, arrival, dc=1)
         copy.wait_recv()
         whole.append(copy)
 
@@ -164,7 +167,7 @@
     def fill_weights():
         load_win.wait()
         load_wout.wait()
-        wih[...], wil[...] = split(win[...].reshape(wih.shape))
+        wih[...], wil[...] = split(win[...].reshape(woh.shape).T)
         woh[...], wol[...] = split(wout[...].reshape(woh.shape))
 
     def fill_combine():
@@ -172,33 +175,58 @@
         combine = row_exp / jnp.sum(row_exp, axis=1, keepdims=True)
         put(jnp.concatenate([combine, jnp.zeros((pad, n_slots), F32)], axis=0).T)
         order = [every_kth(2 * b + a) for a in range(2) for b in range(NY)]
-        ch[...], cl[...] = split(jnp.concatenate(order, axis=0).T[:tokens])
+        by_token = jnp.concatenate(order, axis=0).T[:tokens]
+        first, second = by_token[:, : n_slots // 2], by_token[:, n_slots // 2 :]
+        oh[...], ol[...] = split(jnp.where(c == 0, first, second))
+        ch[...], cl[...] = split(jnp.where(c == 0, second, first))
 
     def flat(a):
-        return a.reshape(-1, WIDE)
-
-    def keep(ref, parts):
-        total, block = merged([flat(a) for a in parts])
-        ref[..., :HALF] = total.reshape(*ref.shape[:-1], HALF)
-        ref[..., HALF:] = block.reshape(*ref.shape[:-1], 128)
+        return a.reshape(-1, a.shape[-1])
+
+    def joined(p, at):
+        return merged([unpacked(flat(sums[(p, c, *at)])), unpacked(flat(recv_c[(p, *at)]))])
+
+    def keep(ref, notes, triple):
+        total, peak, mass = triple
+        ref[...] = total.reshape(ref.shape)
+        groups = total.shape[0] // NZ
+        lane, wide = group_lanes(groups, NZ)
+        block = None
+        for g in range(groups):
+            rows = slice(g * NZ, (g + 1) * NZ)
+            own = jnp.where(lane < 64, peak[rows], mass[rows])
+            block = own if g == 0 else jnp.where(lane % 64 // wide == g, own, block)
+        notes[...] = block
+
+    def noted(ref, notes):
+        total, block = flat(ref[...]), notes[...]
+        groups = total.shape[0] // NZ
+        wide = 64 // groups
+        peak, mass = (
+            jnp.concatenate([block[:, at + wide * g : at + wide * g + 1] for g in range(groups)], axis=0)
+            for at in (0, 64)
+        )
+        return total, peak, mass
 
     sends[0].wait_recv()
-    for dy in ys:
+    for dy in reversed(ys):
         to = lax.rem(y + dy, NY)
-        keep(kept.at[0, to], [sums[0, c, to], recv_c[0, to]])
+        keep(kept.at[0, to], notes_a.at[to], joined(0, (to,)))
+        remote(notes_a.at[to], came_a.at[dy - 1], 13, 18, dy=dy).start()
         remote(kept.at[0, to], recv_a.at[dy - 1], 2, dy=dy).start()
     sends[1].wait_recv()
-    for dx in xs:
+    for dx in reversed(xs):
         to = lax.rem(x + dx, NX)
-        keep(kept.at[1, :, to], [sums[1, c, :, to], recv_c[1, :, to]])
+        keep(kept.at[1, :, to], notes_b.at[to], joined(1, (slice(None), to)))
+        remote(notes_b.at[to], came_b.at[dx - 1], 14, 19, dx=dx).start()
         remote(kept.at[1, :, to], recv_b.at[dx - 1], 3, dx=dx).start()
-    keep(kept.at[0, y], [sums[0, c, y], recv_c[0, y]])
-    keep(kept.at[1, :, x], [sums[1, c, :, x], recv_c[1, :, x]])
+    keep(kept.at[0, y], notes_a.at[y], joined(0, (y,)))
+    keep(kept.at[1, :, x], notes_b.at[x], joined(1, (slice(None), x)))
     fill_weights()
 
-    def to_owners(rows, own, received, got, group, plane, n, at, axis):
-        total, block = merged([flat(a) for a in [own, *received]])
-        total = jnp.concatenate([total, block], axis=1)
+    def to_owners(rows, parts, got, group, plane, n, at, axis):
+        total, peak, mass = merged(parts)
+        total = jnp.concatenate([total, peak_or_mass(peak, mass, n * NZ)], axis=1)
         for i in range(n * NZ):
             rows[i // NZ, i % NZ] = total[i : i + 1]
         for d, dz in plane:
@@ -206,28 +234,32 @@
             remote(src, got.at[d * NZ + dz], group, **{axis: d}, dz=dz).start()
         got[0] = rows[at, z]
 
+    one_wait(13, came_a, 18)
     one_wait(2, recv_a)
+    one_wait(14, came_b, 19)
     one_wait(3, recv_b)
-    to_owners(rows_a, kept[0, y], [recv_a[d] for d in range(NY - 1)], got_a, 4, plane_a, NX, x, "dx")
-    to_owners(rows_b, kept[1, :, x], [recv_b[d] for d in range(NX - 1)], got_b, 5, plane_b, NY, y, "dy")
+    parts = [noted(kept.at[0, y], notes_a.at[y])] + [noted(recv_a.at[d], came_a.at[d]) for d in range(NY - 1)]
+    to_owners(rows_a, parts, got_a, 4, plane_a, NX, x, "dx")
+    parts = [noted(kept.at[1, :, x], notes_b.at[x])] + [noted(recv_b.at[d], came_b.at[d]) for d in range(NX - 1)]
+    to_owners(rows_b, parts, got_b, 5, plane_b, NY, y, "dy")
     fill_combine()
 
     one_wait(4, got_a.at[1:])
     one_wait(5, got_b.at[1:])
     k = y * 2 + c
     for p, got in enumerate((got_a, got_b)):
-        part = got[...].reshape(-1, WIDE)
-        own = part[:, HALF : HALF + 1]
-        total = jnp.sum(part * jnp.exp(own - jnp.max(own, axis=0, keepdims=True)), axis=0, keepdims=True)
-        inputs[k, :, HALF * p : HALF * (p + 1)] = total[:, :HALF] / total[:, HALF + 64 : HALF + 65]
+        total, peak, mass = unpacked(got[...].reshape(-1, WIDE))
+        scale = jnp.exp(peak - jnp.max(peak, axis=0, keepdims=True))
+        total, mass = (jnp.sum(a * scale, axis=0, keepdims=True) for a in (total, mass))
+        inputs[k, :, HALF * p : HALF * (p + 1)] = total / mass
 
     for dy, dc in column:
         remote(inputs.at[k], inputs.at[k], 6, dy=dy, dc=dc).start()
     one_wait(6, inputs.at[1:])
     s_hi, s_lo = split(inputs[...].reshape(K, width))
-    units = wih.shape[0]
-    both = dot(jnp.concatenate([s_hi, s_lo], axis=0), wih[...], TRANSPOSED)
-    v = both[:K] + (both[K:] + dot(s_hi, wil[...], TRANSPOSED))
+    units = wih.shape[1]
+    both = dot(jnp.concatenate([s_hi, s_lo], axis=0), wih[...])
+    v = both[:K] + (both[K:] + dot(s_hi, wil[...]))
     slot = lax.broadcasted_iota(jnp.int32, v.shape, 0)
     unit = lax.broadcasted_iota(jnp.int32, v.shape, 1)
     own = slot // SLOTS == unit // (units // (K // SLOTS))
@@ -244,8 +276,8 @@
     total = osend[k]
     for i in range(len(column)):
         total += orecv[i]
-    own_out[0] = total[:, :HALF]
-    own_out[1] = total[:, HALF:]
+    out_a[...] = total[:, :FIRST]
+    out_b[...] = total[:, FIRST:]
 
     def to_plane(src, everything, group, plane, at, axis):
         row = at * NZ + z
@@ -253,55 +285,60 @@
             remote(src, everything.at[row], group, **{axis: d}, dz=dz).start()
         everything[row] = src[...]
 
-    to_plane(own_out.at[0], all_a, 8, plane_a, x, "dx")
-    to_plane(own_out.at[1], all_b, 9, plane_b, y, "dy")
-
-    def block(p, d=0):
+    to_plane(out_a, all_a, 8, plane_a, x, "dx")
+    to_plane(out_b, all_b, 9, plane_b, y, "dy")
+
+    def block(p, d, own=True):
         if p == 0:
-            return full.at[0, c, lax.rem(y + NY - d, NY)]
-        return full.at[1, c, :, lax.rem(x + NX - d, NX)]
+            return (own_a if own else their_a).at[lax.rem(y + NY - d, NY)]
+        return (own_b if own else their_b).at[:, lax.rem(x + NX - d, NX)]
+
+    def pass_on(p, d):
+        remote(block(p, d), block(p, d, False), 12 + 3 * p, 17 + 3 * p, dc=1).start()
 
     def spread(p, ds, axis):
         copies = {}
         for d in ds:
-            copies[d] = remote(block(p), block(p), 10 + p, 10 + 3 * p + d, **{axis: d})
+            copies[d] = remote(block(p, 0), block(p, 0), 10 + p, 10 + 3 * p + d, **{axis: d})
             copies[d].start()
-        remote(block(p), block(p), 12, 17, dc=1).start()
+        pass_on(p, 0)
         return copies
 
     one_wait(8, all_a.at[1:])
-    full[0, c, y] = all_a[...].reshape(NX, NZ, HALF)
+    own_a[y] = all_a[...].reshape(NX, NZ, FIRST)
     last_a = spread(0, ys, "dy")
     one_wait(9, all_b.at[1:])
-    full[1, c, :, x] = all_b[...].reshape(NY, NZ, HALF)
+    own_b[:, x] = all_b[...].reshape(NY, NZ, own_b.shape[-1])
     last_b = spread(1, xs, "dx")
     for d in reversed(ys):
         last_a[d].wait_recv()
-        remote(block(0, d), block(0, d), 12, 17, dc=1).start()
+        pass_on(0, d)
     for d in reversed(xs):
         last_b[d].wait_recv()
-        remote(block(1, d), block(1, d), 12, 17, dc=1).start()
-    theirs = full.at[:, other]
-    remote(theirs, theirs, 12, 17, dc=1).wait()
+        pass_on(1, d)
+    mixed[:, :FIRST] = dot3(oh[...], ol[...], *split(flat(own_a[...])))
+    mixed[:, FIRST:] = dot3(oh[...], ol[...], *split(flat(own_b[...])))
+    one_wait(12, their_a, 17)
+    one_wait(15, their_b, 20)
     for copy in sends + whole:
         copy.wait_send()
-    three_a, three_b = full.at[0, c, 1:], full.at[1, c, :, 1:]
+    three_a, three_b = own_a.at[1:], own_b.at[:, 1:]
     remote(three_a, three_a, 10, dc=1).wait_send()
     remote(three_b, three_b, 11, dc=1).wait_send()
 
 
-def mix_kernel(full, ch, cl, out_hbm, out, sem):
+def mix_kernel(their_a, their_b, mixed, ch, cl, out_hbm, out, sem):
     copies = []
-    n_slots = ch.shape[1]
-    for p in range(2):
-        f_hi, f_lo = split(full[p].reshape(n_slots, HALF))
-        for start, end in ((0, 256), (256, 512), (512, 640)) if p == 0 else ((0, 128), (128, 384), (384, 640)):
-            at = slice(HALF * p + start, HALF * p + end)
-            out[:, at] = dot3(ch[...], cl[...], f_hi[:, start:end], f_lo[:, start:end])
-            if at.stop % 256 == 0:
-                done = pl.ds(at.stop - 256, 256)
-                copies.append(pltpu.make_async_copy(out.at[:, done], out_hbm.at[:, done], sem.at[len(copies)]))
-                copies[-1].start()
+    start = 0
+    for part in (their_a, their_b):
+        f_hi, f_lo = split(part[...].reshape(-1, part.shape[-1]))
+        for i in range(0, part.shape[-1], 256):
+            at = slice(start + i, start + i + 256)
+            out[:, at] = mixed[:, at] + dot3(ch[...], cl[...], f_hi[:, i : i + 256], f_lo[:, i : i + 256])
+            done = pl.ds(at.start, 256)
+            copies.append(pltpu.make_async_copy(out.at[:, done], out_hbm.at[:, done], sem.at[len(copies)]))
+            copies[-1].start()
+        start += part.shape[-1]
     for copy in copies:
         copy.wait()
 
@@ -318,27 +355,32 @@
     scratch = [
         vmem((T, D), F32), vmem((D, n_slots), F32), vmem((E, H, D), F32), vmem((E, H, D), F32),
         vmem((padded, D), BF16), vmem((padded, D), BF16),
-        vmem((E * H, D), BF16), vmem((E * H, D), BF16), vmem((E * H, D), BF16), vmem((E * H, D), BF16),
+        vmem((D, E * H), BF16), vmem((D, E * H), BF16), vmem((E * H, D), BF16), vmem((E * H, D), BF16),
         vmem((padded // 128, n_slots, 128), F32), vmem((n_slots, 128), F32),
         vmem((n_slots, padded), BF16), vmem((n_slots, padded), BF16),
-        vmem((2, 2, NY, NX, NZ, WIDE), F32), vmem((2, NY, NX, NZ, WIDE), F32), vmem((2, NY, NX, NZ, WIDE), F32),
-        vmem((NY - 1, NX, NZ, WIDE), F32), vmem((NX - 1, NY, NZ, WIDE), F32),
+        vmem((2, 2, NY, NX, NZ, WIDE), F32), vmem((2, NY, NX, NZ, WIDE), F32), vmem((2, NY, NX, NZ, HALF), F32),
+        vmem((NY, NZ, 128), F32), vmem((NX, NZ, 128), F32), vmem((NY - 1, NZ, 128), F32), vmem((NX - 1, NZ, 128), F32),
+        vmem((NY - 1, NX, NZ, HALF), F32), vmem((NX - 1, NY, NZ, HALF), F32),
         vmem((NX, NZ, 1, WIDE), F32), vmem((NY, NZ, 1, WIDE), F32),
         vmem((NX * NZ, 1, WIDE), F32), vmem((NY * NZ, 1, WIDE), F32),
-        vmem((K, 1, D), F32), vmem((K, 1, D), F32), vmem((K - 1, 1, D), F32), vmem((2, 1, HALF), F32),
-        vmem((NX * NZ, 1, HALF), F32), vmem((NY * NZ, 1, HALF), F32),
+        vmem((K, 1, D), F32), vmem((K, 1, D), F32), vmem((K - 1, 1, D), F32), vmem((1, FIRST), F32), vmem((1, D - FIRST), F32),
+        vmem((NX * NZ, 1, FIRST), F32), vmem((NY * NZ, 1, D - FIRST), F32),
+        vmem((NY, NX, NZ, FIRST), F32), vmem((NY, NX, NZ, D - FIRST), F32),
+        vmem((T, n_slots // 2), BF16), vmem((T, n_slots // 2), BF16),
     ]
-    scratch += [dma((2 * (D // 256) + 2,)), dma((13,)), dma((18,))]
+    scratch += [dma((2 * (D // 256) + 2,)), dma((16,)), dma((21,))]
     args = [pltpu.with_memory_space_constraint(a, pltpu.MemorySpace.HBM) for a in (tokens, slot_params, w_in, w_out)]
-    full, ch, cl = pl.pallas_call(
+    results = pl.pallas_call(
         functools.partial(layer_kernel, NX, NY, NZ, stop),
         out_shape=(
-            jax.ShapeDtypeStruct((2, 2, NY, NX, NZ, HALF), F32),
-            jax.ShapeDtypeStruct((T, n_slots), BF16),
-            jax.ShapeDtypeStruct((T, n_slots), BF16),
+            jax.ShapeDtypeStruct((NY, NX, NZ, FIRST), F32),
+            jax.ShapeDtypeStruct((NY, NX, NZ, D - FIRST), F32),
+            jax.ShapeDtypeStruct((T, D), F32),
+            jax.ShapeDtypeStruct((T, n_slots // 2), BF16),
+            jax.ShapeDtypeStruct((T, n_slots // 2), BF16),
         ),
         in_specs=[anywhere] * 4,
-        out_specs=(pl.BlockSpec(memory_space=pltpu.VMEM),) * 3,
+        out_specs=(pl.BlockSpec(memory_space=pltpu.VMEM),) * 5,
         scratch_shapes=scratch,
         compiler_params=pltpu.CompilerParams(
             collective_id=0, has_side_effects=True, vmem_limit_bytes=40 * 1024 * 1024
@@ -348,12 +390,12 @@
     return pl.pallas_call(
         mix_kernel,
         out_shape=jax.ShapeDtypeStruct((T, D), F32),
-        in_specs=[pl.BlockSpec(memory_space=pltpu.VMEM)] * 3,
+        in_specs=[pl.BlockSpec(memory_space=pltpu.VMEM)] * 5,
         out_specs=anywhere,
         scratch_shapes=[vmem((T, D), F32), dma((D // 256,))],
         compiler_params=pltpu.CompilerParams(vmem_limit_bytes=16 * 1024 * 1024),
         name="mix",
-    )(full, ch, cl)
+    )(*results)
 
 
 def solution(mesh, NX=4, NY=4, NZ=8, stop=99):

time: 52.3 us -> 51.1 us (0.977)
  Pallas kernels: 52.2 us -> 51.1 us
    pallas_call x1, Pallas kernels: 50.7 us -> 49.6 us  [body(): pl.pallas_call(functools.partial(layer_kernel, NX, NY, NZ, stop), out_sha...]
where the time goes in v4:
time: 51.1 us
  Pallas kernels  51.1 us (100%)
    pallas_call x1, Pallas kernels, body(): pl.pallas_call(functools.partial(layer_kernel, NX, NY, NZ, stop), out_sha...  49.6 us
    pallas_call x1, Pallas kernels, body(): pl.pallas_call(mix_kernel, out_shape=jax.ShapeDtypeStruct((T, D), F32), i...  1.43 us

profile of v4, /device:TPU:1, one launch (start us, length us, event | category | flops | bytes accessed | tf_op | source)
XLA Modules:
  0.0 51.1 jit_solution(6115510343323252235)
XLA Ops:
  0.0 49.6 %layer.1 = (f32[4,4,8,768]{3,2,1,0:T(8,128)S(1)}, f32[4,4,8,512]{3,2,1,0:T(8,128)S(1)}, f32[224,1280]{1,0:T(8,128)S(1)}, bf16[224,128]{1,0:T(8,128)(2,1)S(1)}, bf16[224,128]{1,0:T(8,128)(2,1)S(1)}) custom-call(f32[224,1280]{1,0:T(8,128)} %tok_hbm.1, f32[1280,256]{1,0:T(8,128)} %par_hbm.1, f32[2,320,1280]{2,1,0:T(8,128)} %win_hbm.1, f32[2,320,1280]{2,1,0:T(8,128)} %wout_hbm.1), custom_call_target="tpu_custom_call" | custom-call | tf_op jit(solution)/shard_map/layer/pallas_call | solution.py:373
  49.6 1.4 %mix.1 = f32[224,1280]{1,0:T(8,128)} custom-call(f32[4,4,8,768]{3,2,1,0:T(8,128)S(1)} %get-tuple-element.10.their_a, f32[4,4,8,512]{3,2,1,0:T(8,128)S(1)} %get-tuple-element.11.their_b, f32[224,1280]{1,0:T(8,128)S(1)} %get-tuple-element.12.mixed, bf16[224,128]{1,0:T(8,128)(2,1)S(1)} %get-tuple-element.13.ch, bf16[224,128]{1,0:T(8,128)(2,1)S(1)} %get-tuple-element.14.cl), custom_call_target="tpu_custom_call" | custom-call | tf_op jit(solution)/shard_map/mix/pallas_call | solution.py:390

commit v5 on v4

--- a/solution.py
+++ b/solution.py
@@ -55,7 +55,7 @@
     NX, NY, NZ, stop,
     tok_hbm, par_hbm, win_hbm, wout_hbm, their_a, their_b, mixed, ch, cl,
     tok, par, win, wout, xh, xl, wih, wil, woh, wol,
-    tmp, ext, wth, wtl, sums, recv_c, kept, notes_a, notes_b, came_a, came_b,
+    tmp, ext, wth, wtl, sums, recv_c, kept, scales, notes_a, notes_b, came_a, came_b,
     recv_a, recv_b, rows_a, rows_b, got_a, got_b, inputs, osend, orecv, out_a, out_b, all_a, all_b, own_a, own_b, oh, ol,
     ld, sent, came,
 ):
@@ -183,20 +183,33 @@
     def flat(a):
         return a.reshape(-1, a.shape[-1])
 
-    def joined(p, at):
-        return merged([unpacked(flat(sums[(p, c, *at)])), unpacked(flat(recv_c[(p, *at)]))])
-
-    def keep(ref, notes, triple):
-        total, peak, mass = triple
-        ref[...] = total.reshape(ref.shape)
-        groups = total.shape[0] // NZ
-        lane, wide = group_lanes(groups, NZ)
-        block = None
-        for g in range(groups):
-            rows = slice(g * NZ, (g + 1) * NZ)
-            own = jnp.where(lane < 64, peak[rows], mass[rows])
-            block = own if g == 0 else jnp.where(lane % 64 // wide == g, own, block)
-        notes[...] = block
+    def packed(blocks):
+        lane, wide = group_lanes(len(blocks), NZ)
+        packet = blocks[0]
+        for g, own in enumerate(blocks):
+            packet = jnp.where(lane % 64 // wide == g, own, packet)
+        return packet
+
+    def fill_scales():
+        ours, theirs = flat(sums[0, c, :, :, :, HALF:]), flat(recv_c[0, :, :, :, HALF:])
+        top = jnp.maximum(ours[:, :1], theirs[:, :1])
+        mass = None
+        for i, part in enumerate((ours, theirs)):
+            scale = jnp.exp(part[:, :1] - top)
+            scales[i] = jnp.broadcast_to(scale, part.shape).reshape(NY, NX, NZ, 128)
+            own = part[:, 64:65] * scale
+            mass = own if mass is None else mass + own
+        block = peak_or_mass(top, mass, top.shape[0])
+        tiles = [[block[(yi * NX + xi) * NZ : (yi * NX + xi + 1) * NZ] for xi in range(NX)] for yi in range(NY)]
+        for yi in range(NY):
+            notes_a[yi] = packed(tiles[yi])
+        for xi in range(NX):
+            notes_b[xi] = packed([tiles[yi][xi] for yi in range(NY)])
+
+    def keep(p, *at):
+        both = (sums[(p, c, *at)], recv_c[(p, *at)])
+        scaled = [a[..., :HALF] * jnp.concatenate([scales[(i, *at)]] * (HALF // 128), axis=-1) for i, a in enumerate(both)]
+        kept[(p, *at)] = scaled[0] + scaled[1]
 
     def noted(ref, notes):
         total, block = flat(ref[...]), notes[...]
@@ -209,19 +222,24 @@
         return total, peak, mass
 
     sends[0].wait_recv()
+    fill_scales()
     for dy in reversed(ys):
         to = lax.rem(y + dy, NY)
-        keep(kept.at[0, to], notes_a.at[to], joined(0, (to,)))
         remote(notes_a.at[to], came_a.at[dy - 1], 13, 18, dy=dy).start()
+    for dx in reversed(xs):
+        to = lax.rem(x + dx, NX)
+        remote(notes_b.at[to], came_b.at[dx - 1], 14, 19, dx=dx).start()
+    for dy in reversed(ys):
+        to = lax.rem(y + dy, NY)
+        keep(0, to)
         remote(kept.at[0, to], recv_a.at[dy - 1], 2, dy=dy).start()
     sends[1].wait_recv()
     for dx in reversed(xs):
         to = lax.rem(x + dx, NX)
-        keep(kept.at[1, :, to], notes_b.at[to], joined(1, (slice(None), to)))
-        remote(notes_b.at[to], came_b.at[dx - 1], 14, 19, dx=dx).start()
+        keep(1, slice(None), to)
         remote(kept.at[1, :, to], recv_b.at[dx - 1], 3, dx=dx).start()
-    keep(kept.at[0, y], notes_a.at[y], joined(0, (y,)))
-    keep(kept.at[1, :, x], notes_b.at[x], joined(1, (slice(None), x)))
+    keep(0, y)
+    keep(1, slice(None), x)
     fill_weights()
 
     def to_owners(rows, parts, got, group, plane, n, at, axis):
@@ -235,11 +253,11 @@
         got[0] = rows[at, z]
 
     one_wait(13, came_a, 18)
+    one_wait(14, came_b, 19)
     one_wait(2, recv_a)
-    one_wait(14, came_b, 19)
-    one_wait(3, recv_b)
     parts = [noted(kept.at[0, y], notes_a.at[y])] + [noted(recv_a.at[d], came_a.at[d]) for d in range(NY - 1)]
     to_owners(rows_a, parts, got_a, 4, plane_a, NX, x, "dx")
+    one_wait(3, recv_b)
     parts = [noted(kept.at[1, :, x], notes_b.at[x])] + [noted(recv_b.at[d], came_b.at[d]) for d in range(NX - 1)]
     to_owners(rows_b, parts, got_b, 5, plane_b, NY, y, "dy")
     fill_combine()
@@ -358,7 +376,7 @@
         vmem((D, E * H), BF16), vmem((D, E * H), BF16), vmem((E * H, D), BF16), vmem((E * H, D), BF16),
         vmem((padded // 128, n_slots, 128), F32), vmem((n_slots, 128), F32),
         vmem((n_slots, padded), BF16), vmem((n_slots, padded), BF16),
-        vmem((2, 2, NY, NX, NZ, WIDE), F32), vmem((2, NY, NX, NZ, WIDE), F32), vmem((2, NY, NX, NZ, HALF), F32),
+        vmem((2, 2, NY, NX, NZ, WIDE), F32), vmem((2, NY, NX, NZ, WIDE), F32), vmem((2, NY, NX, NZ, HALF), F32), vmem((2, NY, NX, NZ, 128), F32),
         vmem((NY, NZ, 128), F32), vmem((NX, NZ, 128), F32), vmem((NY - 1, NZ, 128), F32), vmem((NX - 1, NZ, 128), F32),
         vmem((NY - 1, NX, NZ, HALF), F32), vmem((NX - 1, NY, NZ, HALF), F32),
         vmem((NX, NZ, 1, WIDE), F32), vmem((NY, NZ, 1, WIDE), F32),

time: 51.1 us -> 51 us (level)
  no operation moved by 1% of the time
where the time goes in v5:
time: 51 us
  Pallas kernels  51 us (100%)
    pallas_call x1, Pallas kernels, body(): pl.pallas_call(functools.partial(layer_kernel, NX, NY, NZ, stop), out_sha...  49.5 us
    pallas_call x1, Pallas kernels, body(): pl.pallas_call(mix_kernel, out_shape=jax.ShapeDtypeStruct((T, D), F32), i...  1.43 us

profile of v5, /device:TPU:1, one launch (start us, length us, event | category | flops | bytes accessed | tf_op | source)
XLA Modules:
  0.0 51.0 jit_solution(538261483436407225)
XLA Ops:
  0.0 49.5 %layer.1 = (f32[4,4,8,768]{3,2,1,0:T(8,128)S(1)}, f32[4,4,8,512]{3,2,1,0:T(8,128)S(1)}, f32[224,1280]{1,0:T(8,128)S(1)}, bf16[224,128]{1,0:T(8,128)(2,1)S(1)}, bf16[224,128]{1,0:T(8,128)(2,1)S(1)}) custom-call(f32[224,1280]{1,0:T(8,128)} %tok_hbm.1, f32[1280,256]{1,0:T(8,128)} %par_hbm.1, f32[2,320,1280]{2,1,0:T(8,128)} %win_hbm.1, f32[2,320,1280]{2,1,0:T(8,128)} %wout_hbm.1), custom_call_target="tpu_custom_call" | custom-call | tf_op jit(solution)/shard_map/layer/pallas_call | solution.py:391
  49.5 1.4 %mix.1 = f32[224,1280]{1,0:T(8,128)} custom-call(f32[4,4,8,768]{3,2,1,0:T(8,128)S(1)} %get-tuple-element.10.their_a, f32[4,4,8,512]{3,2,1,0:T(8,128)S(1)} %get-tuple-element.11.their_b, f32[224,1280]{1,0:T(8,128)S(1)} %get-tuple-element.12.mixed, bf16[224,128]{1,0:T(8,128)(2,1)S(1)} %get-tuple-element.13.ch, bf16[224,128]{1,0:T(8,128)(2,1)S(1)} %get-tuple-element.14.cl), custom_call_target="tpu_custom_call" | custom-call | tf_op jit(solution)/shard_map/mix/pallas_call | solution.py:408

commit v6 on v5

--- a/solution.py
+++ b/solution.py
@@ -53,10 +53,10 @@
 
 def layer_kernel(
     NX, NY, NZ, stop,
-    tok_hbm, par_hbm, win_hbm, wout_hbm, their_a, their_b, mixed, ch, cl,
+    tok_hbm, par_hbm, win_hbm, wout_hbm, their_b, mixed, ch, cl,
     tok, par, win, wout, xh, xl, wih, wil, woh, wol,
     tmp, ext, wth, wtl, sums, recv_c, kept, scales, notes_a, notes_b, came_a, came_b,
-    recv_a, recv_b, rows_a, rows_b, got_a, got_b, inputs, osend, orecv, out_a, out_b, all_a, all_b, own_a, own_b, oh, ol,
+    recv_a, recv_b, rows_a, rows_b, got_a, got_b, inputs, osend, orecv, out_a, out_b, all_a, all_b, own_a, own_b, their_a, oh, ol,
     ld, sent, came,
 ):
     x, z, y_lo, c, y_hi = (lax.axis_index(a) for a in AXES)
@@ -337,6 +337,7 @@
     mixed[:, :FIRST] = dot3(oh[...], ol[...], *split(flat(own_a[...])))
     mixed[:, FIRST:] = dot3(oh[...], ol[...], *split(flat(own_b[...])))
     one_wait(12, their_a, 17)
+    mixed[:, :FIRST] += dot3(ch[...], cl[...], *split(flat(their_a[...])))
     one_wait(15, their_b, 20)
     for copy in sends + whole:
         copy.wait_send()
@@ -345,18 +346,17 @@
     remote(three_b, three_b, 11, dc=1).wait_send()
 
 
-def mix_kernel(their_a, their_b, mixed, ch, cl, out_hbm, out, sem):
-    copies = []
-    start = 0
-    for part in (their_a, their_b):
-        f_hi, f_lo = split(part[...].reshape(-1, part.shape[-1]))
-        for i in range(0, part.shape[-1], 256):
-            at = slice(start + i, start + i + 256)
-            out[:, at] = mixed[:, at] + dot3(ch[...], cl[...], f_hi[:, i : i + 256], f_lo[:, i : i + 256])
-            done = pl.ds(at.start, 256)
-            copies.append(pltpu.make_async_copy(out.at[:, done], out_hbm.at[:, done], sem.at[len(copies)]))
-            copies[-1].start()
-        start += part.shape[-1]
+def mix_kernel(their_b, mixed, ch, cl, out_hbm, out, sem):
+    ready = pl.ds(0, FIRST)
+    copies = [pltpu.make_async_copy(mixed.at[:, ready], out_hbm.at[:, ready], sem.at[0])]
+    copies[0].start()
+    f_hi, f_lo = split(their_b[...].reshape(-1, their_b.shape[-1]))
+    for i in range(0, out.shape[1], 256):
+        at = pl.ds(FIRST + i, 256)
+        part = dot3(ch[...], cl[...], f_hi[:, i : i + 256], f_lo[:, i : i + 256])
+        out[:, i : i + 256] = mixed[:, FIRST + i : FIRST + i + 256] + part
+        copies.append(pltpu.make_async_copy(out.at[:, pl.ds(i, 256)], out_hbm.at[:, at], sem.at[len(copies)]))
+        copies[-1].start()
     for copy in copies:
         copy.wait()
 
@@ -383,7 +383,7 @@
         vmem((NX * NZ, 1, WIDE), F32), vmem((NY * NZ, 1, WIDE), F32),
         vmem((K, 1, D), F32), vmem((K, 1, D), F32), vmem((K - 1, 1, D), F32), vmem((1, FIRST), F32), vmem((1, D - FIRST), F32),
         vmem((NX * NZ, 1, FIRST), F32), vmem((NY * NZ, 1, D - FIRST), F32),
-        vmem((NY, NX, NZ, FIRST), F32), vmem((NY, NX, NZ, D - FIRST), F32),
+        vmem((NY, NX, NZ, FIRST), F32), vmem((NY, NX, NZ, D - FIRST), F32), vmem((NY, NX, NZ, FIRST), F32),
         vmem((T, n_slots // 2), BF16), vmem((T, n_slots // 2), BF16),
     ]
     scratch += [dma((2 * (D // 256) + 2,)), dma((16,)), dma((21,))]
@@ -391,14 +391,13 @@
     results = pl.pallas_call(
         functools.partial(layer_kernel, NX, NY, NZ, stop),
         out_shape=(
-            jax.ShapeDtypeStruct((NY, NX, NZ, FIRST), F32),
             jax.ShapeDtypeStruct((NY, NX, NZ, D - FIRST), F32),
             jax.ShapeDtypeStruct((T, D), F32),
             jax.ShapeDtypeStruct((T, n_slots // 2), BF16),
             jax.ShapeDtypeStruct((T, n_slots // 2), BF16),
         ),
         in_specs=[anywhere] * 4,
-        out_specs=(pl.BlockSpec(memory_space=pltpu.VMEM),) * 5,
+        out_specs=(pl.BlockSpec(memory_space=pltpu.VMEM),) * 4,
         scratch_shapes=scratch,
         compiler_params=pltpu.CompilerParams(
             collective_id=0, has_side_effects=True, vmem_limit_bytes=40 * 1024 * 1024
@@ -408,9 +407,9 @@
     return pl.pallas_call(
         mix_kernel,
         out_shape=jax.ShapeDtypeStruct((T, D), F32),
-        in_specs=[pl.BlockSpec(memory_space=pltpu.VMEM)] * 5,
+        in_specs=[pl.BlockSpec(memory_space=pltpu.VMEM)] * 4,
         out_specs=anywhere,
-        scratch_shapes=[vmem((T, D), F32), dma((D // 256,))],
+        scratch_shapes=[vmem((T, D - FIRST), F32), dma((1 + (D - FIRST) // 256,))],
         compiler_params=pltpu.CompilerParams(vmem_limit_bytes=16 * 1024 * 1024),
         name="mix",
     )(*results)

time: 51 us -> 50.9 us (level)
  no operation moved by 1% of the time
where the time goes in v6:
time: 50.9 us
  Pallas kernels  50.9 us (100%)
    pallas_call x1, Pallas kernels, body(): pl.pallas_call(functools.partial(layer_kernel, NX, NY, NZ, stop), out_sha...  49.7 us
    pallas_call x1, Pallas kernels, body(): pl.pallas_call(mix_kernel, out_shape=jax.ShapeDtypeStruct((T, D), F32), i...  1.13 us

profile of v6, /device:TPU:1, one launch (start us, length us, event | category | flops | bytes accessed | tf_op | source)
XLA Modules:
  0.0 50.9 jit_solution(8460749669622017551)
XLA Ops:
  0.0 49.7 %layer.1 = (f32[4,4,8,512]{3,2,1,0:T(8,128)S(1)}, f32[224,1280]{1,0:T(8,128)S(1)}, bf16[224,128]{1,0:T(8,128)(2,1)S(1)}, bf16[224,128]{1,0:T(8,128)(2,1)S(1)}) custom-call(f32[224,1280]{1,0:T(8,128)} %tok_hbm.1, f32[1280,256]{1,0:T(8,128)} %par_hbm.1, f32[2,320,1280]{2,1,0:T(8,128)} %win_hbm.1, f32[2,320,1280]{2,1,0:T(8,128)} %wout_hbm.1), custom_call_target="tpu_custom_call" | custom-call | tf_op jit(solution)/shard_map/layer/pallas_call | solution.py:391
  49.7 1.1 %mix.1 = f32[224,1280]{1,0:T(8,128)} custom-call(f32[4,4,8,512]{3,2,1,0:T(8,128)S(1)} %get-tuple-element.9.their_b, f32[224,1280]{1,0:T(8,128)S(1)} %get-tuple-element.10.mixed, bf16[224,128]{1,0:T(8,128)(2,1)S(1)} %get-tuple-element.11.ch, bf16[224,128]{1,0:T(8,128)(2,1)S(1)} %get-tuple-element.12.cl), custom_call_target="tpu_custom_call" | custom-call | tf_op jit(solution)/shard_map/mix/pallas_call | solution.py:407
